TPU v7x, 512 devices: a whole 4x8x8 slice. The times are simulated.
512 devices in a mesh: gx: 32 (over y, x), gy: 16 (over z, core).
Axes of the slice: x: 4, y: 8, z: 8, core: 2. Of those that a mesh axis runs over, the one named last changes fastest.
Arguments:
- hidden_in: bfloat16 [4096, 2560], P('gx'), may hold values from -48 to 48
- norm_gain: bfloat16 [2560], replicated, may hold values from 0.099609375 to 1.8984375
- router_weight: bfloat16 [2560, 64], replicated, may hold values from -3 to 3
- routes: int32 [4096, 6], P('gx'), may hold values from 0 to 63, as said below
- w_gate_up: bfloat16 [512, 2560, 384], P(('gx', 'gy')), may hold values from -0.125 to 0.125
- w_down: bfloat16 [512, 192, 2560], P(('gx', 'gy')), may hold values from -0.15625 to 0.15625
- final_gain: bfloat16 [2560], replicated, may hold values from 0.099609375 to 1.8984375
- head_weight: bfloat16 [2560, 53248], P('gy', 'gx'), may hold values from -5 to 5
- targets: int32 [4096], replicated, may hold values from 0 to 53247
Outputs:
- logprob: float32 [32, 128], P(None, 'gy')
- entropy: float32 [32, 128], P(None, 'gy')
Inputs may be any that keep to these rules, and one draw needn't show every extreme that they name: `routes`: each row names 6 different experts. Within the 128 rows of one index of gx no expert is named by more than 16 rows, and one expert, the same for every index of gx, is named by exactly 16 rows in each.
All inputs are finite; a program needn't handle non-finite values.
Results may differ from a plain program's by a relative error of at most 0.012.
Values may be sent and summed in bfloat16 or wider, within the bound.
A program may use at most 192 MiB of HBM per device.

v0:
```python
import jax
import jax.numpy as jnp
from jax import lax
from jax.sharding import PartitionSpec as P

SPLITS = 8


NORM_EPSILON = 1e-06


def rms_scale(values, gain_vector):
    widened = values.astype(jnp.float32)
    return (
        widened
        * lax.rsqrt(jnp.mean(widened * widened, -1, keepdims=True) + NORM_EPSILON)
        * gain_vector.astype(jnp.float32)
    )


def finish(peak_value, total_mass, spread, target_logit):
    log_mass = jnp.log(total_mass)
    return (target_logit - peak_value - log_mass, log_mass - spread / total_mass)


def shards(
    hidden_in, norm_gain, router_weight, routes, w_gate_up, w_down, final_gain, head_weight, targets
):
    tok_rows = hidden_in.shape[0]
    group_count = lax.axis_size("gx")
    lane_count = lax.axis_size("gy")
    group_index = lax.axis_index("gx")
    lane_index = lax.axis_index("gy")
    expert_count = router_weight.shape[1]
    held_slices = w_gate_up.shape[0]
    unit_count = w_down.shape[1]
    slot_count = tok_rows // 8
    share_rows = tok_rows // lane_count
    columns = head_weight.shape[1]
    normed = rms_scale(hidden_in, norm_gain).astype(jnp.bfloat16)
    scores = jnp.dot(normed, router_weight, preferred_element_type=jnp.float32)
    chosen = routes[:, :, None] == jnp.arange(expert_count, dtype=jnp.int32)[None, None, :]
    picked = jnp.sum(jnp.where(chosen, scores[:, None, :], 0.0), -1)
    gate_values = jax.nn.softmax(picked, axis=-1).astype(jnp.bfloat16)
    gate_table = jnp.sum(jnp.where(chosen, gate_values.astype(jnp.float32)[:, :, None], 0.0), 1)
    member = jnp.sum(chosen.astype(jnp.int32), 1)
    slot_rank = jnp.cumsum(member, 0) - member
    slot_hit = (member[:, :, None] == 1) & (
        slot_rank[:, :, None] == jnp.arange(slot_count, dtype=jnp.int32)[None, None, :]
    )
    lane_slices = (
        jnp.arange(group_count, dtype=jnp.int32)[:, None] * lane_count + lane_index
    ) * held_slices + jnp.arange(held_slices, dtype=jnp.int32)[None, :]
    owner_expert = lane_slices // SPLITS
    pick_expert = (
        owner_expert[:, :, None] == jnp.arange(expert_count, dtype=jnp.int32)[None, None, :]
    ).astype(jnp.bfloat16)
    dispatch = jnp.einsum(
        "tke,nec->tkcn",
        pick_expert,
        slot_hit.astype(jnp.bfloat16),
        preferred_element_type=jnp.float32,
    ).astype(jnp.bfloat16)
    outgoing = jnp.einsum(
        "tkcn,nd->tkcd", dispatch, normed, preferred_element_type=jnp.float32
    ).astype(jnp.bfloat16)
    expert_gate = jnp.einsum(
        "tke,ne->tkn",
        pick_expert,
        gate_table.astype(jnp.bfloat16),
        preferred_element_type=jnp.float32,
    )
    combine = (dispatch.astype(jnp.float32) * expert_gate[:, :, None, :]).astype(jnp.bfloat16)
    lifted = jnp.einsum(
        "skcd,kdf->skcf",
        lax.all_to_all(outgoing, "gx", split_axis=0, concat_axis=0, tiled=True),
        w_gate_up,
        preferred_element_type=jnp.float32,
    )
    active = (jax.nn.silu(lifted[..., :unit_count]) * lifted[..., unit_count:]).astype(jnp.bfloat16)
    result = jnp.einsum(
        "skcf,kfd->skcd", active, w_down, preferred_element_type=jnp.float32
    ).astype(jnp.bfloat16)
    returned = lax.all_to_all(result, "gx", split_axis=0, concat_axis=0, tiled=True)
    partial_value = jnp.einsum(
        "tkcn,tkcd->nd", combine, returned, preferred_element_type=jnp.float32
    )
    summed = lax.psum_scatter(partial_value, "gy", scatter_dimension=0, tiled=True)
    residual = lax.dynamic_slice_in_dim(hidden_in, lane_index * share_rows, share_rows, 0)
    layer_out = (residual.astype(jnp.float32) + summed).astype(jnp.bfloat16)
    final_states = rms_scale(layer_out, final_gain).astype(jnp.bfloat16)
    gathered = lax.all_gather(final_states, "gx", axis=0, tiled=True)
    target_grid = targets.reshape(group_count, tok_rows)
    logits = jnp.dot(
        gathered,
        lax.all_gather(head_weight, "gy", axis=0, tiled=True),
        preferred_element_type=jnp.float32,
    )
    offset = group_index * columns
    own_targets = lax.dynamic_slice_in_dim(
        target_grid, lane_index * share_rows, share_rows, 1
    ).reshape(group_count * share_rows)
    target_hits = (offset + jnp.arange(columns, dtype=jnp.int32))[None, :] == own_targets[:, None]
    peak_value = lax.pmax(jnp.max(logits, -1), "gx")
    shifted = logits - peak_value[:, None]
    weights = jnp.exp(shifted)
    total_mass, spread, target_logit = lax.psum(
        (
            jnp.sum(weights, -1),
            jnp.sum(weights * shifted, -1),
            jnp.sum(jnp.where(target_hits, logits, 0.0), -1),
        ),
        "gx",
    )
    logprob, entropy = finish(peak_value, total_mass, spread, target_logit)
    return (logprob.reshape(group_count, share_rows), entropy.reshape(group_count, share_rows))


def solution(mesh):
    return jax.shard_map(
        shards,
        mesh=mesh,
        in_specs=(
            P("gx", None),
            P(),
            P(),
            P("gx", None),
            P(("gx", "gy"), None, None),
            P(("gx", "gy"), None, None),
            P(),
            P("gy", "gx"),
            P(),
        ),
        out_specs=(P(None, "gy"), P(None, "gy")),
        check_vma=False,
    )
```

profile of v0, /device:TPU:2, one launch (start us, length us, event | category | flops | bytes accessed | tf_op | source)
XLA Modules:
  0.0 525.7 jit_solution(14808827266614481248)
XLA Ops:
  7.2 0.0 copy-start
  7.2 0.0 copy-start.1
  7.2 0.9 convert_reduce_fusion
  8.1 0.1 copy.35
  8.2 0.7 convert_element_type.89
  8.9 1.3 fusion.8
  10.2 0.2 reduce_window_sum.11
  10.4 0.1 copy.37
  10.4 0.3 convolution_convert_fusion.2
  10.7 0.0 copy-done.1
  10.7 0.9 fusion.1
  11.7 71.8 %all_to_all.10 = bf16[32,1,16,2560]{3,2,1,0:T(8,128)(2,1)S(1)} all-to-all(bf16[32,1,16,2560]{3,2,1,0:T(8,128)(2,1)S(1)} %fusion.1), channel_id=1, replica_groups=mesh['gx'=32,'gy'=16] {'gx'}, dimensions={0} | all-to-all | bytes 5242880 | tf_op jit(solution)/shard_map/all_to_all | solution.py:76
  83.5 0.0 copy-done
  83.5 0.0 copy-start.5
  83.5 1.5 fusion.11
  85.0 0.0 copy-done.5
  85.0 2.4 fusion
  87.5 0.0 copy-start.6
  87.5 5.8 %all-to-all-start.1 = ((bf16[32,1,16,2560]{3,2,1,0:T(8,128)(2,1)}), bf16[32,1,16,2560]{3,2,1,0:T(8,128)(2,1)}, u32[]{:S(2)}, u32[]{:S(2)}) async-start(bf16[32,1,16,2560]{3,2,1,0:T(8,128)(2,1)} %fusion), calls=%async_computation.1 | async-start | bytes 5242880 | tf_op jit(solution)/shard_map/all_to_all | solution.py:84
  93.3 0.0 reduce-scatter.2.cloned.1.call-start
  93.3 0.0 copy-done.6
  93.3 0.4 fusion.26
  93.8 0.0 copy-done.2
  93.9 0.2 fusion.36
  94.1 58.5 %all-to-all-done.1 = bf16[32,1,16,2560]{3,2,1,0:T(8,128)(2,1)} async-done(((bf16[32,1,16,2560]{3,2,1,0:T(8,128)(2,1)}), bf16[32,1,16,2560]{3,2,1,0:T(8,128)(2,1)}, u32[]{:S(2)}, u32[]{:S(2)}) %all-to-all-start.1) | async-done | bytes 2621472 | tf_op jit(solution)/shard_map/all_to_all | solution.py:84
  152.6 4.5 convolution_bitcast_fusion
  157.1 0.0 reduce-scatter.2.cloned.1.call-update
  157.1 0.0 all-gather.3.cloned.1.call-start
  157.2 0.0 copy-done.4
  157.2 62.9 %reduce-scatter.2.cloned.1.call-done = f32[8,2560]{1,0:T(8,128)} async-done(((f32[128,2560]{1,0:T(8,128)}), f32[8,2560]{1,0:T(8,128)}) %reduce-scatter.2.cloned.1.call-update) | async-done | bytes 81936 | tf_op jit(solution)/shard_map/reduce_scatter | solution.py:88
  220.1 1.0 fusion.33
  221.1 0.7 fusion.35
  221.8 0.0 all-gather.3.cloned.1.call-update
  221.8 0.0 all-gather.5.cloned.1.call-start
  221.9 0.7 all-gather.5.cloned.1.call-update
  222.6 0.0 copy-done.3
  222.6 0.1 constant_dynamic-slice_fusion
  222.7 0.1 eq.70
  222.8 79.2 %all-gather.3.cloned.1.call-done = bf16[256,2560]{1,0:T(8,128)(2,1)} async-done(((bf16[8,2560]{1,0:T(8,128)(2,1)}), bf16[256,2560]{1,0:T(8,128)(2,1)}) %all-gather.3.cloned.1.call-update) | async-done | bytes 1310736 | tf_op jit(solution)/shard_map/all_gather | solution.py:92
  301.9 61.2 %all-gather.5.cloned.1.call-done = bf16[2560,1664]{1,0:T(8,128)(2,1)} async-done(((bf16[160,1664]{1,0:T(8,128)(2,1)}), bf16[2560,1664]{1,0:T(8,128)(2,1)}) %all-gather.5.cloned.1.call-update) | async-done | bytes 8519696 | tf_op jit(solution)/shard_map/all_gather | solution.py:96
  363.1 7.6 %fusion.45 = (f32[256]{0:T(256)S(1)}, f32[256,1664]{1,0:T(8,128)}) fusion(bf16[256,2560]{1,0:T(8,128)(2,1)} %all-gather.3.cloned.1.call-done, bf16[2560,1664]{1,0:T(8,128)(2,1)} %all-gather.5.cloned.1.call-done), kind=kOutput, calls=%fused_computation.68 | convolution fusion | flops 2181463808 | bytes 11535360 | tf_op jit(solution)/shard_map/dot_general | solution.py:94
  370.7 70.6 %pmax.7 = f32[256]{0:T(256)S(1)} all-reduce(f32[256]{0:T(256)S(1)} %get-tuple-element.18), channel_id=1, replica_groups=mesh['gx'=32,'gy'=16] {'gx'}, use_global_device_ids=true, to_apply=%region_12.13 | all-reduce | flops 256 | bytes 2048 | tf_op jit(solution)/shard_map/pmax | solution.py:104
  441.4 2.1 fusion.7
  443.5 74.1 %all-reduce = (f32[256]{0:T(256)S(1)}, f32[256]{0:T(256)S(1)}, f32[256]{0:T(256)S(1)}) all-reduce(f32[256]{0:T(256)S(1)} %get-tuple-element.10, f32[256]{0:T(256)S(1)} %get-tuple-element.9, f32[256]{0:T(256)S(1)} %get-tuple-element.8), channel_id=1, replica_groups=mesh['gx'=32,'gy'=16] {'gx'}, use_global_device_ids=true, to_apply=%region_10.11 | all-reduce | flops 768 | bytes 6144 | tf_op jit(solution)/shard_map/psum | solution.py:107
  517.6 0.1 reshape.187
  517.7 0.7 copy.42
  518.4 0.1 reshape.188
  518.5 0.7 copy.43
  (16 shorter events, 0.2 us)
Async XLA Ops:
  7.2 76.3 %copy-start = (bf16[1,2560,384]{2,1,0:T(8,128)(2,1)S(1)}, bf16[1,2560,384]{2,1,0:T(8,128)(2,1)}, u32[]{:S(2)}) copy-start(bf16[1,2560,384]{2,1,0:T(8,128)(2,1)} %param.13) | copy-start | bytes 5898244
  7.2 3.5 copy-start.1
  83.5 1.5 copy-start.5
  87.5 5.8 %copy-start.6 = (bf16[2560,64]{0,1:T(8,128)(2,1)S(1)}, bf16[2560,64]{0,1:T(8,128)(2,1)}, u32[]{:S(2)}) copy-start(bf16[2560,64]{0,1:T(8,128)(2,1)} %param.11) | copy-start | bytes 983044
  87.5 6.3 %copy-start.2 = (s32[128,6]{0,1:T(8,128)S(1)}, s32[128,6]{0,1:T(8,128)}, u32[]{:S(2)}) copy-start(s32[128,6]{0,1:T(8,128)} %param.12) | copy-start | bytes 9220
  87.5 65.1 %all-to-all-start.1 = ((bf16[32,1,16,2560]{3,2,1,0:T(8,128)(2,1)}), bf16[32,1,16,2560]{3,2,1,0:T(8,128)(2,1)}, u32[]{:S(2)}, u32[]{:S(2)}) async-start(bf16[32,1,16,2560]{3,2,1,0:T(8,128)(2,1)} %fusion), calls=%async_computation.1 | async-start | bytes 5242880 | tf_op jit(solution)/shard_map/all_to_all | solution.py:84
  93.3 126.8 %reduce-scatter.2.cloned.1.call-start = ((), (), s32[]{:S(2)}) async-start(), calls=%async_computation.3 | async-start | bytes 1392640 | tf_op jit(solution)/shard_map/reduce_scatter | solution.py:88
  94.1 63.1 %copy-start.4 = (bf16[2560]{0:T(1024)(128)(2,1)S(1)}, bf16[2560]{0:T(1024)(128)(2,1)}, u32[]{:S(2)}) copy-start(bf16[2560]{0:T(1024)(128)(2,1)} %param.15) | copy-start | bytes 15364
  157.1 65.5 %copy-start.3 = (s32[4096]{0:T(1024)S(1)}, s32[4096]{0:T(1024)}, u32[]{:S(2)}) copy-start(s32[4096]{0:T(1024)} %param.17) | copy-start | bytes 49156
  157.1 144.8 %all-gather.3.cloned.1.call-start = ((), (), s32[]{:S(2)}) async-start(), calls=%async_computation.4 | async-start | bytes 1351680 | tf_op jit(solution)/shard_map/all_gather | solution.py:92
  221.8 141.3 %all-gather.5.cloned.1.call-start = ((), (), s32[]{:S(2)}) async-start(), calls=%async_computation.5 | async-start | bytes 9052160 | tf_op jit(solution)/shard_map/all_gather | solution.py:96
Sparse Core Ops, SparseCore 0:
  157.2 62.7 reduce-scatter.1
  223.2 78.6 all-gather.2
  304.1 59.0 all-gather.4
where the time goes:
time: 526 us
  waiting for transfers between devices  262 us (50%)
  blocking collectives  217 us (41%)
  matrix products  17.9 us (3%)
  between operations  13.9 us (3%)
  other arithmetic  7.05 us (1%)
  starting transfers between devices  5.9 us (1%)
    all_gather x1, waiting for transfers between devices, shards(): gathered = lax.all_gather(final_states, 'gx', axis=0, tiled=True)  79.2 us
    psum x1, blocking collectives, shards(): lax.psum((jnp.sum(weights, -1), jnp.sum(weights * shifted, -1), jnp.sum(j...  74.1 us
    all_to_all x1, blocking collectives, shards(): lax.all_to_all(outgoing, 'gx', split_axis=0, concat_axis=0, tiled=True)  71.8 us
    pmax x1, blocking collectives, shards(): peak_value = lax.pmax(jnp.max(logits, -1), 'gx')  70.6 us
    reduce_scatter x1, waiting for transfers between devices, shards(): lax.psum_scatter(partial_value, 'gy', scatter_dimension=0, tiled=True)  62.9 us
    all_gather x1, waiting for transfers between devices, shards(): lax.all_gather(head_weight, 'gy', axis=0, tiled=True)  61.2 us
    all_to_all x1, waiting for transfers between devices, shards(): lax.all_to_all(result, 'gx', split_axis=0, concat_axis=0, tiled=True)  58.5 us
  transfers between devices with their start and end apart: 4, of which 4 were waited for; matrix products, arithmetic and copies ran while one was open for 0% of the time, Pallas kernels for 0%

commit v1 on v0

v1 whole, which is shorter than its diff:
```python
import functools

import jax
import jax.numpy as jnp
from jax import lax
from jax.experimental import pallas as pl
from jax.experimental.pallas import tpu as pltpu
from jax.sharding import PartitionSpec as P

SPLITS = 8
X_CHIPS = 4

NORM_EPSILON = 1e-06

VMEM = pl.BlockSpec(memory_space=pltpu.VMEM)
ANY = pl.BlockSpec(memory_space=pl.ANY)


def rms_scale(values, gain_vector):
    widened = values.astype(jnp.float32)
    return (
        widened
        * lax.rsqrt(jnp.mean(widened * widened, -1, keepdims=True) + NORM_EPSILON)
        * gain_vector.astype(jnp.float32)
    )


def remote(src, dst, send_sem, recv_sem, device):
    return pltpu.make_async_remote_copy(
        src_ref=src,
        dst_ref=dst,
        send_sem=send_sem,
        recv_sem=recv_sem,
        device_id=device,
        device_id_type=pl.DeviceIdType.MESH,
    )


def greet(devices):
    barrier = pltpu.get_barrier_semaphore()
    for device in devices:
        pl.semaphore_signal(
            barrier, inc=1, device_id=device, device_id_type=pl.DeviceIdType.MESH
        )
    pl.semaphore_wait(barrier, len(devices))


def offsets(axis, count):
    if axis == "gy":
        steps = [1]
        for z in range(1, count // 4 + 1):
            for sign in (1, -1):
                if sign == 1 or 2 * z != count // 2:
                    steps += [(sign * z, 0), (sign * z, 1)]
        return steps
    y_chips = count // X_CHIPS
    steps = []
    for y in range(0, y_chips // 2 + 1):
        for x in range(X_CHIPS):
            for sign in (1, -1):
                if (y == 0 or 2 * y == y_chips) and sign == -1:
                    continue
                if y or x:
                    steps.append((sign * y, x))
    return steps


def partners(axis, count, me):
    if axis == "gy":
        chips = count // 2
        z, core = me // 2, lax.rem(me, 2)
        found = [me + 1 - 2 * core]
        for step in offsets(axis, count)[1:]:
            found.append(
                lax.rem(z + step[0] + chips, chips) * 2 + lax.rem(core + step[1], 2)
            )
        return found
    y_chips = count // X_CHIPS
    y, x = me // X_CHIPS, lax.rem(me, X_CHIPS)
    return [
        lax.rem(y + dy + y_chips, y_chips) * X_CHIPS + lax.rem(x + dx, X_CHIPS)
        for dy, dx in offsets(axis, count)
    ]


def exchange_kernel(axis, same, count, *refs):
    src, out, send_sem, recv_sem, own_sem = refs
    me = lax.axis_index(axis)
    others = partners(axis, count, me)
    greet([{axis: other} for other in others])
    copies = [
        remote(
            src if same else src.at[other],
            out.at[me],
            send_sem.at[other],
            recv_sem.at[me],
            {axis: other},
        )
        for other in others
    ]
    for copy in copies:
        copy.start()
    own = pltpu.make_async_copy(src if same else src.at[me], out.at[me], own_sem)
    own.start()
    own.wait()
    for other in others:
        remote(
            src if same else src.at[other],
            out.at[other],
            send_sem.at[other],
            recv_sem.at[other],
            {axis: other},
        ).wait_recv()
    for copy in copies:
        copy.wait_send()


def exchange(values, axis, collective_id, same=False):
    count = lax.axis_size(axis)
    shape = (count,) + values.shape if same else values.shape
    return pl.pallas_call(
        functools.partial(exchange_kernel, axis, same, count),
        out_shape=jax.ShapeDtypeStruct(shape, values.dtype),
        in_specs=[VMEM],
        out_specs=VMEM,
        scratch_shapes=[
            pltpu.SemaphoreType.DMA((count,)),
            pltpu.SemaphoreType.DMA((count,)),
            pltpu.SemaphoreType.DMA,
        ],
        compiler_params=pltpu.CompilerParams(collective_id=collective_id, has_side_effects=True),
        cost_estimate=pl.CostEstimate(
            flops=0, bytes_accessed=40_000_000, transcendentals=0
        ),
    )(values)


def dispatch_kernel(count, *refs):
    (src, up, down, out, other_up, other_down, send_sem, recv_sem, own_sem, pair_sems) = refs
    me = lax.axis_index("gx")
    lane = lax.axis_index("gy")
    others = partners("gx", count, me)
    pair = {"gy": lane + 1 - 2 * lax.rem(lane, 2)}
    greet([pair] + [{"gx": other} for other in others])
    copies = [
        remote(
            src.at[other], out.at[me], send_sem.at[other], recv_sem.at[me], {"gx": other}
        )
        for other in others
    ]
    swaps = [
        remote(up, other_up, pair_sems.at[0], pair_sems.at[1], pair),
        remote(down, other_down, pair_sems.at[2], pair_sems.at[3], pair),
    ]
    for copy in copies:
        copy.start()
    for copy in swaps:
        copy.start()
    own = pltpu.make_async_copy(src.at[me], out.at[me], own_sem)
    own.start()
    own.wait()
    for other in others:
        remote(
            src.at[other], out.at[other], send_sem.at[other], recv_sem.at[other], {"gx": other}
        ).wait_recv()
    for copy in copies:
        copy.wait_send()
    for copy in swaps:
        copy.wait()


def dispatch_rows(values, up, down, collective_id):
    count = lax.axis_size("gx")
    return pl.pallas_call(
        functools.partial(dispatch_kernel, count),
        out_shape=(
            jax.ShapeDtypeStruct(values.shape, values.dtype),
            jax.ShapeDtypeStruct(up.shape, up.dtype),
            jax.ShapeDtypeStruct(down.shape, down.dtype),
        ),
        in_specs=[VMEM, ANY, ANY],
        out_specs=(VMEM, ANY, ANY),
        scratch_shapes=[
            pltpu.SemaphoreType.DMA((count,)),
            pltpu.SemaphoreType.DMA((count,)),
            pltpu.SemaphoreType.DMA,
            pltpu.SemaphoreType.DMA((4,)),
        ],
        compiler_params=pltpu.CompilerParams(collective_id=collective_id, has_side_effects=True),
        cost_estimate=pl.CostEstimate(
            flops=0, bytes_accessed=100_000_000, transcendentals=0
        ),
    )(values, up, down)


def relay_kernel(count, *refs):
    src, out, send_sem, recv_sem, own_sem = refs
    me = lax.axis_index("gx")
    y_chips = count // X_CHIPS
    y, x = me // X_CHIPS, lax.rem(me, X_CHIPS)

    def at(row, column):
        return lax.rem(row + y_chips, y_chips) * X_CHIPS + lax.rem(column, X_CHIPS)

    above, below = at(y + 1, x), at(y - 1, x)
    sides = [at(y, x + 1), at(y, x + 3), at(y, x + 2)]
    greet([{"gx": other} for other in [above, below] + sides])
    sent = []

    def send(block, source, target):
        copy = remote(
            source, out.at[block], send_sem.at[len(sent)], recv_sem.at[block], {"gx": target}
        )
        copy.start()
        sent.append(copy)

    def arrived(block):
        remote(
            src, out.at[block], send_sem.at[0], recv_sem.at[block], {"gx": above}
        ).wait_recv()

    send(me, src, above)
    send(me, src, below)
    for side in sides:
        send(me, src, side)
    own = pltpu.make_async_copy(src, out.at[me], own_sem)
    own.start()
    half = y_chips // 2
    for step in range(1, half + 1):
        block = at(y - step, x)
        arrived(block)
        if step < half:
            send(block, out.at[block], above)
        for side in sides:
            send(block, out.at[block], side)
        if step < half:
            block = at(y + step, x)
            arrived(block)
            if step < half - 1:
                send(block, out.at[block], below)
            for side in sides:
                send(block, out.at[block], side)
    for row in range(y_chips):
        for column in range(1, X_CHIPS):
            arrived(at(y + row, x + column))
    own.wait()
    for copy in sent:
        copy.wait_send()


def relay_gather(values, collective_id):
    count = lax.axis_size("gx")
    return pl.pallas_call(
        functools.partial(relay_kernel, count),
        out_shape=jax.ShapeDtypeStruct((count,) + values.shape, values.dtype),
        in_specs=[VMEM],
        out_specs=VMEM,
        scratch_shapes=[
            pltpu.SemaphoreType.DMA((count,)),
            pltpu.SemaphoreType.DMA((count,)),
            pltpu.SemaphoreType.DMA,
        ],
        compiler_params=pltpu.CompilerParams(collective_id=collective_id, has_side_effects=True),
        cost_estimate=pl.CostEstimate(
            flops=0, bytes_accessed=40_000_000, transcendentals=0
        ),
    )(values)


def shards(
    hidden_in, norm_gain, router_weight, routes, w_gate_up, w_down, final_gain, head_weight, targets
):
    tok_rows = hidden_in.shape[0]
    width = hidden_in.shape[1]
    group_count = lax.axis_size("gx")
    lane_count = lax.axis_size("gy")
    group_index = lax.axis_index("gx")
    lane_index = lax.axis_index("gy")
    expert_count = router_weight.shape[1]
    unit_count = w_down.shape[1]
    slot_count = tok_rows // 16
    share_rows = tok_rows // lane_count
    columns = head_weight.shape[1]
    head_full = lax.all_gather(head_weight, "gy", axis=0, tiled=True)
    normed = rms_scale(hidden_in, norm_gain).astype(jnp.bfloat16)
    scores = jnp.dot(normed, router_weight, preferred_element_type=jnp.float32)
    chosen = routes[:, :, None] == jnp.arange(expert_count, dtype=jnp.int32)[None, None, :]
    picked = jnp.sum(jnp.where(chosen, scores[:, None, :], 0.0), -1)
    gate_values = jax.nn.softmax(picked, axis=-1).astype(jnp.bfloat16)
    gate_table = jnp.sum(jnp.where(chosen, gate_values.astype(jnp.float32)[:, :, None], 0.0), 1)
    member = jnp.sum(chosen.astype(jnp.int32), 1)
    slot_rank = jnp.cumsum(member, 0) - member
    slot_base = lax.rem(lane_index, 2) * slot_count
    slot_hit = (member[:, :, None] == 1) & (
        slot_rank[:, :, None] == slot_base + jnp.arange(slot_count, dtype=jnp.int32)[None, None, :]
    )
    owner_expert = (
        jnp.arange(group_count, dtype=jnp.int32) * lane_count + lane_index
    ) // SPLITS
    pick_expert = (
        owner_expert[:, None] == jnp.arange(expert_count, dtype=jnp.int32)[None, :]
    ).astype(jnp.bfloat16)
    dispatch = jnp.einsum(
        "te,nec->tcn",
        pick_expert,
        slot_hit.astype(jnp.bfloat16),
        preferred_element_type=jnp.float32,
    ).astype(jnp.bfloat16)
    outgoing = jnp.einsum(
        "tcn,nd->tcd", dispatch, normed, preferred_element_type=jnp.float32
    ).astype(jnp.bfloat16)
    expert_gate = jnp.einsum(
        "te,ne->tn",
        pick_expert,
        gate_table.astype(jnp.bfloat16),
        preferred_element_type=jnp.float32,
    )
    combine = (dispatch.astype(jnp.float32) * expert_gate[:, None, :]).astype(jnp.bfloat16)
    own_up, own_down = w_gate_up[0], w_down[0]
    rows, pair_up, pair_down = dispatch_rows(outgoing, own_up, own_down, 1)
    rows = rows.reshape(group_count * slot_count, width)

    def block(up, down):
        lifted = jnp.dot(rows, up, preferred_element_type=jnp.float32)
        active = (
            jax.nn.silu(lifted[:, :unit_count]) * lifted[:, unit_count:]
        ).astype(jnp.bfloat16)
        return jnp.dot(active, down, preferred_element_type=jnp.float32)

    result = (block(own_up, own_down) + block(pair_up, pair_down)).astype(jnp.bfloat16)
    returned = exchange(result.reshape(group_count, slot_count, width), "gx", 2)
    partial_value = jnp.einsum(
        "tcn,tcd->nd", combine, returned, preferred_element_type=jnp.float32
    ).astype(jnp.bfloat16)
    pieces = exchange(partial_value.reshape(lane_count, share_rows, width), "gy", 3)
    summed = jnp.sum(pieces.astype(jnp.float32), 0)
    residual = lax.dynamic_slice_in_dim(hidden_in, lane_index * share_rows, share_rows, 0)
    layer_out = (residual.astype(jnp.float32) + summed).astype(jnp.bfloat16)
    final_states = rms_scale(layer_out, final_gain).astype(jnp.bfloat16)
    gathered = relay_gather(final_states, 4).reshape(group_count * share_rows, width)
    target_grid = targets.reshape(group_count, tok_rows)
    logits = jnp.dot(gathered, head_full, preferred_element_type=jnp.float32)
    offset = group_index * columns
    own_targets = lax.dynamic_slice_in_dim(
        target_grid, lane_index * share_rows, share_rows, 1
    ).reshape(group_count * share_rows)
    target_hits = (offset + jnp.arange(columns, dtype=jnp.int32))[None, :] == own_targets[:, None]
    local_peak = jnp.max(logits, -1)
    shifted = logits - local_peak[:, None]
    weights = jnp.exp(shifted)
    local = jnp.stack(
        [
            local_peak,
            jnp.sum(weights, -1),
            jnp.sum(weights * shifted, -1),
            jnp.sum(jnp.where(target_hits, logits, 0.0), -1),
        ]
    )
    stats = exchange(local, "gx", 5, same=True)
    peaks, masses, spreads = stats[:, 0], stats[:, 1], stats[:, 2]
    peak_value = jnp.max(peaks, 0)
    below = peaks - peak_value[None, :]
    scale = jnp.exp(below)
    total_mass = jnp.sum(masses * scale, 0)
    spread = jnp.sum(scale * (spreads + below * masses), 0)
    log_mass = jnp.log(total_mass)
    logprob = jnp.sum(stats[:, 3], 0) - peak_value - log_mass
    entropy = log_mass - spread / total_mass
    return (logprob.reshape(group_count, share_rows), entropy.reshape(group_count, share_rows))


def solution(mesh):
    return jax.shard_map(
        shards,
        mesh=mesh,
        in_specs=(
            P("gx", None),
            P(),
            P(),
            P("gx", None),
            P(("gx", "gy"), None, None),
            P(("gx", "gy"), None, None),
            P(),
            P("gy", "gx"),
            P(),
        ),
        out_specs=(P(None, "gy"), P(None, "gy")),
        check_vma=False,
    )
```

time: 526 us -> 188 us (0.36)
  the two profiles are of different devices: /device:TPU:2 before, /device:TPU:64 now
where the time goes in v1:
time: 188 us
  Pallas kernels  147 us (78%)
  matrix products  15.9 us (8%)
  between operations  14.3 us (8%)
  other arithmetic  6.72 us (4%)
  local copies, waits for them, and re-layouts  3.5 us (2%)
    pallas_call x3, Pallas kernels, exchange(): pl.pallas_call(functools.partial(exchange_kernel, axis, same, count), out...  81.9 us
    pallas_call x1, Pallas kernels, dispatch_rows(): pl.pallas_call(functools.partial(dispatch_kernel, count), out_shape=(jax....  38.9 us
    pallas_call x1, Pallas kernels, relay_gather(): pl.pallas_call(functools.partial(relay_kernel, count), out_shape=jax.Shap...  25.8 us
    dot_general x1, matrix products, shards(): logits = jnp.dot(gathered, head_full, preferred_element_type=jnp.float32)  6.45 us
  transfers between devices with their start and end apart: 1, of which 0 were waited for; matrix products, arithmetic and copies ran while one was open for 7% of the time, Pallas kernels for 71%

profile of v1, /device:TPU:64, one launch (start us, length us, event | category | flops | bytes accessed | tf_op | source)
XLA Modules:
  0.0 187.8 jit_solution(18158540829623833906)
XLA Ops:
  7.2 0.0 copy-start
  7.2 0.0 copy-start.5
  7.2 0.0 all-gather.2.cloned.1.call-start
  7.2 0.7 all-gather.2.cloned.1.call-update
  7.9 0.7 convert_reduce_fusion.1
  8.6 0.1 copy.29
  8.7 0.2 reduce_window_sum.11
  8.9 0.1 copy.31
  9.0 0.7 convert_element_type.82
  9.7 0.2 fusion.5
  10.0 0.2 fusion.15
  10.2 1.7 convolution_convert_fusion.refs_0_
  11.9 38.9 %shard_map.104 = (bf16[32,8,2560]{2,1,0:T(8,128)(2,1)}, bf16[2560,384]{1,0:T(8,128)(2,1)}, bf16[192,2560]{1,0:T(8,128)(2,1)}) custom-call(bf16[32,8,2560]{2,1,0:T(8,128)(2,1)} %convolution_convert_fusion.refs_0_, bf16[2560,384]{1,0:T(8,128)(2,1)} %bitcast.64, bf16[192,2560]{1,0:T(8,128)(2,1)} %bitcast.65), custom_call_target="tpu_custom_call" | custom-call | bytes 100000000 | tf_op jit(solution)/shard_map/pallas_call | solution.py:174
  50.9 0.0 copy-done.1
  50.9 0.0 copy-start.2
  50.9 0.0 copy-start.6
  50.9 2.3 %fusion.12 = f32[256,384]{1,0:T(8,128)S(1)} fusion(bf16[32,8,2560]{2,1,0:T(8,128)(2,1)} %get-tuple-element.5, bf16[1,2560,384]{2,1,0:T(8,128)(2,1)S(1)} %copy-done.1), kind=kOutput, calls=%fused_computation.20 | convolution fusion | flops 503316480 | bytes 3670016 | tf_op jit(solution)/shard_map/dot_general | solution.py:324
  53.2 0.1 copy-done.6
  53.3 0.9 fusion.10
  54.2 0.3 copy-done.4
  54.5 0.6 fusion.24
  55.1 0.6 copy-done.7
  55.7 1.7 fusion.1.refs_0_
  57.4 40.2 %shard_map.105 = bf16[32,8,2560]{2,1,0:T(8,128)(2,1)} custom-call(bf16[32,8,2560]{2,1,0:T(8,128)(2,1)} %fusion.1.refs_0_), custom_call_target="tpu_custom_call" | custom-call | bytes 40000000 | tf_op jit(solution)/shard_map/pallas_call | solution.py:121
  97.6 0.0 copy-start.8
  97.7 0.4 fusion.22
  98.1 0.3 copy-done.8
  98.5 0.2 fusion.40
  98.6 0.3 copy-done.3
  99.0 1.5 fusion.3.refs_0_
  100.4 28.1 %shard_map.106 = bf16[16,8,2560]{2,1,0:T(8,128)(2,1)} custom-call(bf16[16,8,2560]{2,1,0:T(8,128)(2,1)} %fusion.3.refs_0_), custom_call_target="tpu_custom_call" | custom-call | bytes 40000000 | tf_op jit(solution)/shard_map/pallas_call | solution.py:121
  128.6 0.0 copy-start.9
  128.6 1.2 convert_reduce_fusion
  129.8 0.1 fusion.32
  129.9 0.7 fusion.34.refs_0_
  130.6 25.8 %shard_map.107 = bf16[32,8,2560]{2,1,0:T(8,128)(2,1)} custom-call(bf16[8,2560]{1,0:T(8,128)(2,1)} %fusion.34.refs_0_), custom_call_target="tpu_custom_call" | custom-call | bytes 40000000 | tf_op jit(solution)/shard_map/pallas_call | solution.py:253
  156.5 0.1 constant_dynamic-slice_fusion
  156.6 0.1 eq.77
  156.7 0.0 all-gather.2.cloned.1.call-done
  156.7 6.4 %fusion.53 = (f32[256]{0:T(256)S(1)}, f32[256,1664]{1,0:T(8,128)S(1)}) fusion(bf16[2560,1664]{1,0:T(8,128)(2,1)} %all-gather.2.cloned.1.call-done, bf16[32,8,2560]{2,1,0:T(8,128)(2,1)} %shard_map.107), kind=kOutput, calls=%fused_computation.90 | convolution fusion | flops 2181463808 | bytes 11535360 | tf_op jit(solution)/shard_map/dot_general | solution.py:342
  163.1 0.8 exponential_reduce_fusion
  163.9 0.6 pad_maximum_fusion.refs_0_
  164.5 13.5 %shard_map.108 = f32[32,4,256]{2,1,0:T(4,128)} custom-call(f32[4,256]{1,0:T(4,128)} %pad_maximum_fusion.refs_0_), custom_call_target="tpu_custom_call" | custom-call | bytes 40000000 | tf_op jit(solution)/shard_map/pallas_call | solution.py:121
  178.1 1.3 fusion.52
  179.4 0.1 sub.70
  179.5 0.7 copy.36
  180.2 0.1 sub.72
  180.2 0.7 copy.37
  (25 shorter events, 0.2 us)
Async XLA Ops:
  7.2 90.5 %copy-start = (bf16[2560,64]{0,1:T(8,128)(2,1)S(1)}, bf16[2560,64]{0,1:T(8,128)(2,1)}, u32[]{:S(2)}) copy-start(bf16[2560,64]{0,1:T(8,128)(2,1)} %param.11) | copy-start | bytes 983044
  7.2 2.6 %copy-start.5 = (bf16[128,2560]{1,0:T(8,128)(2,1)S(1)}, bf16[128,2560]{1,0:T(8,128)(2,1)}, u32[]{:S(2)}) copy-start(bf16[128,2560]{1,0:T(8,128)(2,1)} %param.9) | copy-start | bytes 1966084
  7.2 149.5 %all-gather.2.cloned.1.call-start = ((), (), s32[]{:S(2)}) async-start(), calls=%async_computation | async-start | bytes 9052160 | tf_op jit(solution)/shard_map/all_gather | solution.py:284
  11.9 39.0 %copy-start.1 = (bf16[1,2560,384]{2,1,0:T(8,128)(2,1)S(1)}, bf16[1,2560,384]{2,1,0:T(8,128)(2,1)}, u32[]{:S(2)}) copy-start(bf16[1,2560,384]{2,1,0:T(8,128)(2,1)} %param.13) | copy-start | bytes 5898244
  50.9 2.4 %copy-start.2 = (bf16[32,8,2560]{2,1,0:T(8,128)(2,1)S(1)}, bf16[32,8,2560]{2,1,0:T(8,128)(2,1)}, u32[]{:S(2)}) copy-start(bf16[32,8,2560]{2,1,0:T(8,128)(2,1)} %get-tuple-element.5) | copy-start | bytes 3932164
  50.9 2.4 %copy-start.6 = (bf16[2560,384]{1,0:T(8,128)(2,1)S(1)}, bf16[2560,384]{1,0:T(8,128)(2,1)}, u32[]{:S(2)}) copy-start(bf16[2560,384]{1,0:T(8,128)(2,1)} %get-tuple-element.6) | copy-start | bytes 5898244
  53.3 1.2 copy-start.4
  54.5 1.2 copy-start.7
  97.6 0.7 copy-start.8
  97.6 1.3 copy-start.3
  99.0 29.6 %copy-start.10 = (bf16[2560]{0:T(1024)(128)(2,1)S(1)}, bf16[2560]{0:T(1024)(128)(2,1)}, u32[]{:S(2)}) copy-start(bf16[2560]{0:T(1024)(128)(2,1)} %param.15) | copy-start | bytes 15364
  128.6 27.9 %copy-start.9 = (s32[4096]{0:T(1024)S(1)}, s32[4096]{0:T(1024)}, u32[]{:S(2)}) copy-start(s32[4096]{0:T(1024)} %param.17) | copy-start | bytes 49156
Sparse Core Ops, SparseCore 0:
  10.1 61.4 all-gather.1

commit v2 on v1

--- a/solution.py
+++ b/solution.py
@@ -47,11 +47,9 @@
 
 def offsets(axis, count):
     if axis == "gy":
-        steps = [1]
-        for z in range(1, count // 4 + 1):
-            for sign in (1, -1):
-                if sign == 1 or 2 * z != count // 2:
-                    steps += [(sign * z, 0), (sign * z, 1)]
+        steps = []
+        for z in range(1, count // 2 + 1):
+            steps += [z] if 2 * z == count else [z, -z]
         return steps
     y_chips = count // X_CHIPS
     steps = []
@@ -67,14 +65,7 @@
 
 def partners(axis, count, me):
     if axis == "gy":
-        chips = count // 2
-        z, core = me // 2, lax.rem(me, 2)
-        found = [me + 1 - 2 * core]
-        for step in offsets(axis, count)[1:]:
-            found.append(
-                lax.rem(z + step[0] + chips, chips) * 2 + lax.rem(core + step[1], 2)
-            )
-        return found
+        return [lax.rem(me + step + count, count) for step in offsets(axis, count)]
     y_chips = count // X_CHIPS
     y, x = me // X_CHIPS, lax.rem(me, X_CHIPS)
     return [
@@ -86,15 +77,22 @@
 def exchange_kernel(axis, same, count, *refs):
     src, out, send_sem, recv_sem, own_sem = refs
     me = lax.axis_index(axis)
+    core = 0
+    if axis == "gy":
+        me, core = me // 2, lax.rem(me, 2)
+
+    def device(other):
+        return {axis: 2 * other + core if axis == "gy" else other}
+
     others = partners(axis, count, me)
-    greet([{axis: other} for other in others])
+    greet([device(other) for other in others])
     copies = [
         remote(
             src if same else src.at[other],
             out.at[me],
             send_sem.at[other],
             recv_sem.at[me],
-            {axis: other},
+            device(other),
         )
         for other in others
     ]
@@ -109,14 +107,14 @@
             out.at[other],
             send_sem.at[other],
             recv_sem.at[other],
-            {axis: other},
+            device(other),
         ).wait_recv()
     for copy in copies:
         copy.wait_send()
 
 
 def exchange(values, axis, collective_id, same=False):
-    count = lax.axis_size(axis)
+    count = lax.axis_size(axis) // (2 if axis == "gy" else 1)
     shape = (count,) + values.shape if same else values.shape
     return pl.pallas_call(
         functools.partial(exchange_kernel, axis, same, count),
@@ -135,35 +133,74 @@
     )(values)
 
 
+def relay_roles(count, me):
+    y_chips = count // X_CHIPS
+    y, x = me // X_CHIPS, lax.rem(me, X_CHIPS)
+
+    def at(row, column):
+        return lax.rem(row + y_chips, y_chips) * X_CHIPS + lax.rem(column + X_CHIPS, X_CHIPS)
+
+    half = y_chips // 2
+    sends = [(at(y + half, x + dx), at(y - 1, x + dx)) for dx in (1, 3)]
+    serves = [(at(y + 1, x - dx), at(y + 1 + half, x)) for dx in (1, 3)]
+    direct = [
+        at(y + dy, x + dx)
+        for dy, dx in offsets("gx", count)
+        if not (dy == half and dx in (1, 3))
+    ]
+    everyone = partners("gx", count, me)
+    return sends, serves, direct, everyone
+
+
 def dispatch_kernel(count, *refs):
-    (src, up, down, out, other_up, other_down, send_sem, recv_sem, own_sem, pair_sems) = refs
+    (src, up, down, out, other_up, other_down) = refs[:6]
+    (held, send_sem, recv_sem, own_sem, pair_sems, relay_sems) = refs[6:]
     me = lax.axis_index("gx")
     lane = lax.axis_index("gy")
-    others = partners("gx", count, me)
+    sends, serves, direct, everyone = relay_roles(count, me)
     pair = {"gy": lane + 1 - 2 * lax.rem(lane, 2)}
-    greet([pair] + [{"gx": other} for other in others])
-    copies = [
-        remote(
-            src.at[other], out.at[me], send_sem.at[other], recv_sem.at[me], {"gx": other}
-        )
-        for other in others
-    ]
+    greet([pair] + [{"gx": other} for other in everyone])
+    sent = []
+
+    def send(copy):
+        copy.start()
+        sent.append(copy)
+
+    for k, (target, relay) in enumerate(sends):
+        send(
+            remote(
+                src.at[target], held.at[k], send_sem.at[target], relay_sems.at[k], {"gx": relay}
+            )
+        )
+    for other in direct:
+        send(
+            remote(
+                src.at[other], out.at[me], send_sem.at[other], recv_sem.at[me], {"gx": other}
+            )
+        )
     swaps = [
         remote(up, other_up, pair_sems.at[0], pair_sems.at[1], pair),
         remote(down, other_down, pair_sems.at[2], pair_sems.at[3], pair),
     ]
-    for copy in copies:
-        copy.start()
     for copy in swaps:
         copy.start()
     own = pltpu.make_async_copy(src.at[me], out.at[me], own_sem)
     own.start()
+    for k, (source, target) in enumerate(serves):
+        remote(
+            held.at[k], held.at[k], relay_sems.at[2 + k], relay_sems.at[k], {"gx": target}
+        ).wait_recv()
+        send(
+            remote(
+                held.at[k], out.at[source], relay_sems.at[2 + k], recv_sem.at[source], {"gx": target}
+            )
+        )
     own.wait()
-    for other in others:
+    for other in everyone:
         remote(
             src.at[other], out.at[other], send_sem.at[other], recv_sem.at[other], {"gx": other}
         ).wait_recv()
-    for copy in copies:
+    for copy in sent:
         copy.wait_send()
     for copy in swaps:
         copy.wait()
@@ -181,9 +218,11 @@
         in_specs=[VMEM, ANY, ANY],
         out_specs=(VMEM, ANY, ANY),
         scratch_shapes=[
+            pltpu.VMEM((2,) + values.shape[1:], values.dtype),
             pltpu.SemaphoreType.DMA((count,)),
             pltpu.SemaphoreType.DMA((count,)),
             pltpu.SemaphoreType.DMA,
+            pltpu.SemaphoreType.DMA((4,)),
             pltpu.SemaphoreType.DMA((4,)),
         ],
         compiler_params=pltpu.CompilerParams(collective_id=collective_id, has_side_effects=True),
@@ -193,6 +232,139 @@
     )(values, up, down)
 
 
+def return_kernel(count, *refs):
+    (src, out, held, send_sem, recv_sem, own_sem, relay_sems) = refs
+    me = lax.axis_index("gx")
+    lane = lax.axis_index("gy")
+    core = lax.rem(lane, 2)
+    first = lane - core
+    wide = src.shape[2] // 2
+    sends, serves, direct, everyone = relay_roles(count, me)
+    pair = {"gy": first + 1 - core}
+    greet([pair] + [{"gx": other, "gy": first + c} for other in everyone for c in range(2)])
+    sent = []
+
+    def send(copy):
+        copy.start()
+        sent.append(copy)
+
+    def half(c):
+        return pl.ds(pl.multiple_of(c * wide, 128), wide)
+
+    for k, (target, relay) in enumerate(sends):
+        send(
+            remote(
+                src.at[target],
+                held.at[k],
+                send_sem.at[target, 0],
+                relay_sems.at[k],
+                {"gx": relay},
+            )
+        )
+    for other in direct:
+        for c in range(2):
+            send(
+                remote(
+                    src.at[other, :, half(c)],
+                    out.at[me, core],
+                    send_sem.at[other, c],
+                    recv_sem.at[me, core],
+                    {"gx": other, "gy": first + c},
+                )
+            )
+    send(
+        remote(
+            src.at[me, :, half(1 - core)],
+            out.at[me, core],
+            send_sem.at[me, 0],
+            recv_sem.at[me, core],
+            pair,
+        )
+    )
+    own = pltpu.make_async_copy(src.at[me, :, half(core)], out.at[me, core], own_sem)
+    own.start()
+    for k, (source, target) in enumerate(serves):
+        remote(
+            held.at[k], held.at[k], relay_sems.at[2 + k], relay_sems.at[k], {"gx": target}
+        ).wait_recv()
+        for c in range(2):
+            send(
+                remote(
+                    held.at[k, :, half(c)],
+                    out.at[source, core],
+                    relay_sems.at[2 + 2 * k + c],
+                    recv_sem.at[source, core],
+                    {"gx": target, "gy": first + c},
+                )
+            )
+    own.wait()
+    for other in everyone:
+        for c in range(2):
+            remote(
+                src.at[other, :, half(c)],
+                out.at[other, c],
+                send_sem.at[other, c],
+                recv_sem.at[other, c],
+                {"gx": other},
+            ).wait_recv()
+    remote(
+        src.at[me, :, half(core)],
+        out.at[me, 1 - core],
+        send_sem.at[me, 0],
+        recv_sem.at[me, 1 - core],
+        pair,
+    ).wait_recv()
+    for copy in sent:
+        copy.wait_send()
+
+
+def return_rows(values, collective_id):
+    count = lax.axis_size("gx")
+    slots, width = values.shape[1:]
+    return pl.pallas_call(
+        functools.partial(return_kernel, count),
+        out_shape=jax.ShapeDtypeStruct((count, 2, slots, width // 2), values.dtype),
+        in_specs=[VMEM],
+        out_specs=VMEM,
+        scratch_shapes=[
+            pltpu.VMEM((2, slots, width), values.dtype),
+            pltpu.SemaphoreType.DMA((count, 2)),
+            pltpu.SemaphoreType.DMA((count, 2)),
+            pltpu.SemaphoreType.DMA,
+            pltpu.SemaphoreType.DMA((6,)),
+        ],
+        compiler_params=pltpu.CompilerParams(collective_id=collective_id, has_side_effects=True),
+        cost_estimate=pl.CostEstimate(
+            flops=0, bytes_accessed=40_000_000, transcendentals=0
+        ),
+    )(values)
+
+
+def pair_kernel(src, out, send_sem, recv_sem, own_sem):
+    lane = lax.axis_index("gy")
+    core = lax.rem(lane, 2)
+    pair = {"gy": lane + 1 - 2 * core}
+    greet([pair])
+    copy = remote(src.at[1 - core], out.at[core], send_sem, recv_sem, pair)
+    copy.start()
+    own = pltpu.make_async_copy(src.at[core], out.at[core], own_sem)
+    own.start()
+    own.wait()
+    copy.wait_send()
+    remote(src.at[core], out.at[1 - core], send_sem, recv_sem, pair).wait_recv()
+
+
+def pair_swap(values, collective_id):
+    return pl.pallas_call(
+        pair_kernel,
+        out_shape=jax.ShapeDtypeStruct(values.shape, values.dtype),
+        in_specs=[VMEM],
+        out_specs=VMEM,
+        scratch_shapes=[pltpu.SemaphoreType.DMA] * 3,
+        compiler_params=pltpu.CompilerParams(collective_id=collective_id, has_side_effects=True),
+    )(values)
+
+
 def relay_kernel(count, *refs):
     src, out, send_sem, recv_sem, own_sem = refs
     me = lax.axis_index("gx")
@@ -203,8 +375,8 @@
         return lax.rem(row + y_chips, y_chips) * X_CHIPS + lax.rem(column, X_CHIPS)
 
     above, below = at(y + 1, x), at(y - 1, x)
-    sides = [at(y, x + 1), at(y, x + 3), at(y, x + 2)]
-    greet([{"gx": other} for other in [above, below] + sides])
+    right, left = at(y, x + 1), at(y, x + 3)
+    greet([{"gx": other} for other in (above, below, right, left)])
     sent = []
 
     def send(block, source, target):
@@ -219,30 +391,40 @@
             src, out.at[block], send_sem.at[0], recv_sem.at[block], {"gx": above}
         ).wait_recv()
 
+    def across(k):
+        near, far = (x + 3, right) if k % 2 == 0 else (x + 1, left)
+        block = at(y + k, near)
+        arrived(block)
+        send(block, out.at[block], far)
+
     send(me, src, above)
     send(me, src, below)
-    for side in sides:
-        send(me, src, side)
+    send(me, src, right)
+    send(me, src, left)
     own = pltpu.make_async_copy(src, out.at[me], own_sem)
     own.start()
     half = y_chips // 2
+    order = [0]
     for step in range(1, half + 1):
-        block = at(y - step, x)
-        arrived(block)
+        order.append(y_chips - step)
         if step < half:
-            send(block, out.at[block], above)
-        for side in sides:
-            send(block, out.at[block], side)
-        if step < half:
-            block = at(y + step, x)
+            order.append(step)
+    for i, k in enumerate(order):
+        if k:
+            block = at(y + k, x)
             arrived(block)
-            if step < half - 1:
+            if half < k:
+                send(block, out.at[block], above)
+            elif k < half - 1:
                 send(block, out.at[block], below)
-            for side in sides:
-                send(block, out.at[block], side)
-    for row in range(y_chips):
-        for column in range(1, X_CHIPS):
-            arrived(at(y + row, x + column))
+            send(block, out.at[block], right)
+            send(block, out.at[block], left)
+        if i >= 1:
+            across(order[i - 1])
+    across(order[-1])
+    for k in order:
+        arrived(at(y + k, x + (1 if k % 2 == 0 else 3)))
+        arrived(at(y + k, x + 2))
     own.wait()
     for copy in sent:
         copy.wait_send()
@@ -278,7 +460,8 @@
     lane_index = lax.axis_index("gy")
     expert_count = router_weight.shape[1]
     unit_count = w_down.shape[1]
-    slot_count = tok_rows // 16
+    slot_count = tok_rows // 8
+    half_slots = slot_count // 2
     share_rows = tok_rows // lane_count
     columns = head_weight.shape[1]
     head_full = lax.all_gather(head_weight, "gy", axis=0, tiled=True)
@@ -290,9 +473,8 @@
     gate_table = jnp.sum(jnp.where(chosen, gate_values.astype(jnp.float32)[:, :, None], 0.0), 1)
     member = jnp.sum(chosen.astype(jnp.int32), 1)
     slot_rank = jnp.cumsum(member, 0) - member
-    slot_base = lax.rem(lane_index, 2) * slot_count
     slot_hit = (member[:, :, None] == 1) & (
-        slot_rank[:, :, None] == slot_base + jnp.arange(slot_count, dtype=jnp.int32)[None, None, :]
+        slot_rank[:, :, None] == jnp.arange(slot_count, dtype=jnp.int32)[None, None, :]
     )
     owner_expert = (
         jnp.arange(group_count, dtype=jnp.int32) * lane_count + lane_index
@@ -306,8 +488,10 @@
         slot_hit.astype(jnp.bfloat16),
         preferred_element_type=jnp.float32,
     ).astype(jnp.bfloat16)
+    core = lax.rem(lane_index, 2)
+    own_slots = lax.dynamic_slice_in_dim(dispatch, core * half_slots, half_slots, 1)
     outgoing = jnp.einsum(
-        "tcn,nd->tcd", dispatch, normed, preferred_element_type=jnp.float32
+        "tcn,nd->tcd", own_slots, normed, preferred_element_type=jnp.float32
     ).astype(jnp.bfloat16)
     expert_gate = jnp.einsum(
         "te,ne->tn",
@@ -318,7 +502,7 @@
     combine = (dispatch.astype(jnp.float32) * expert_gate[:, None, :]).astype(jnp.bfloat16)
     own_up, own_down = w_gate_up[0], w_down[0]
     rows, pair_up, pair_down = dispatch_rows(outgoing, own_up, own_down, 1)
-    rows = rows.reshape(group_count * slot_count, width)
+    rows = rows.reshape(group_count * half_slots, width)
 
     def block(up, down):
         lifted = jnp.dot(rows, up, preferred_element_type=jnp.float32)
@@ -328,12 +512,19 @@
         return jnp.dot(active, down, preferred_element_type=jnp.float32)
 
     result = (block(own_up, own_down) + block(pair_up, pair_down)).astype(jnp.bfloat16)
-    returned = exchange(result.reshape(group_count, slot_count, width), "gx", 2)
+    returned = return_rows(result.reshape(group_count, half_slots, width), 2)
     partial_value = jnp.einsum(
-        "tcn,tcd->nd", combine, returned, preferred_element_type=jnp.float32
+        "tcn,tcd->nd",
+        combine,
+        returned.reshape(group_count, slot_count, width // 2),
+        preferred_element_type=jnp.float32,
     ).astype(jnp.bfloat16)
-    pieces = exchange(partial_value.reshape(lane_count, share_rows, width), "gy", 3)
-    summed = jnp.sum(pieces.astype(jnp.float32), 0)
+    chips = lane_count // 2
+    pieces = exchange(partial_value.reshape(chips, 2 * share_rows, width // 2), "gy", 3)
+    halves = pair_swap(
+        jnp.sum(pieces.astype(jnp.float32), 0).reshape(2, share_rows, width // 2), 6
+    )
+    summed = jnp.concatenate([halves[0], halves[1]], axis=-1)
     residual = lax.dynamic_slice_in_dim(hidden_in, lane_index * share_rows, share_rows, 0)
     layer_out = (residual.astype(jnp.float32) + summed).astype(jnp.bfloat16)
     final_states = rms_scale(layer_out, final_gain).astype(jnp.bfloat16)

time: 188 us -> 197 us (1.048)
  Pallas kernels: 147 us -> 154 us
    pallas_call x0 -> x2, Pallas kernels: none -> 46.7 us  [the longest x1 43.3 us: return_rows(): pl.pallas_call(functools.partial(return_kernel, count), out_shape=jax.Sha...]
    pallas_call x3 -> x2, Pallas kernels: 81.9 us -> 36.5 us  [exchange(): pl.pallas_call(functools.partial(exchange_kernel, axis, same, count), out...]
    pallas_call x1, Pallas kernels: 38.9 us -> 44.3 us  [dispatch_rows(): pl.pallas_call(functools.partial(dispatch_kernel, count), out_shape=(jax....]
  transfers between devices with their start and end apart: 1 -> 1, of which waited for: 0 -> 0; matrix products, arithmetic and copies ran while one was open for 7% -> 8% of each run, Pallas kernels for 71% -> 71%
where the time goes in v2:
time: 197 us; the launch traced here: 196 us
  Pallas kernels  154 us (78%)
  matrix products  15.8 us (8%)
  between operations  14.3 us (7%)
  other arithmetic  7.18 us (4%)
  local copies, waits for them, and re-layouts  4.27 us (2%)
    pallas_call x1, Pallas kernels, dispatch_rows(): pl.pallas_call(functools.partial(dispatch_kernel, count), out_shape=(jax....  44.3 us
    pallas_call x1, Pallas kernels, return_rows(): pl.pallas_call(functools.partial(return_kernel, count), out_shape=jax.Sha...  43.3 us
    pallas_call x2, Pallas kernels, exchange(): pl.pallas_call(functools.partial(exchange_kernel, axis, same, count), out...  36.5 us
    pallas_call x1, Pallas kernels, relay_gather(): pl.pallas_call(functools.partial(relay_kernel, count), out_shape=jax.Shap...  26.5 us
    dot_general x1, matrix products, shards(): logits = jnp.dot(gathered, head_full, preferred_element_type=jnp.float32)  6.45 us
  transfers between devices with their start and end apart: 1, of which 0 were waited for; matrix products, arithmetic and copies ran while one was open for 8% of the time, Pallas kernels for 71%

profile of v2, /device:TPU:64, one launch (start us, length us, event | category | flops | bytes accessed | tf_op | source)
XLA Modules:
  0.0 196.4 jit_solution(6037655073949893623)
XLA Ops:
  7.2 0.0 copy-start
  7.2 0.0 all-gather.2.cloned.1.call-start
  7.2 0.7 all-gather.2.cloned.1.call-update
  7.9 0.7 convert_reduce_fusion.1
  8.7 0.1 copy.29
  8.7 0.2 reduce_window_sum.11
  8.9 0.1 copy.31
  9.0 0.7 convert_element_type.83
  9.7 0.2 convolution_convert_fusion.1
  10.0 0.0 copy-done.5
  10.0 0.2 fusion.4
  10.2 1.7 convolution_convert_fusion.refs_0_
  11.9 44.3 %shard_map.104 = (bf16[32,8,2560]{2,1,0:T(8,128)(2,1)}, bf16[2560,384]{1,0:T(8,128)(2,1)}, bf16[192,2560]{1,0:T(8,128)(2,1)}) custom-call(bf16[32,8,2560]{2,1,0:T(8,128)(2,1)} %convolution_convert_fusion.refs_0_, bf16[2560,384]{1,0:T(8,128)(2,1)} %bitcast.72, bf16[192,2560]{1,0:T(8,128)(2,1)} %bitcast.74), custom_call_target="tpu_custom_call" | custom-call | bytes 100000000 | tf_op jit(solution)/shard_map/pallas_call | solution.py:211
  56.3 2.4 %fusion.11 = f32[256,384]{1,0:T(8,128)S(1)} fusion(bf16[32,8,2560]{2,1,0:T(8,128)(2,1)} %get-tuple-element.5, bf16[1,2560,384]{2,1,0:T(8,128)(2,1)S(1)} %copy-done.1), kind=kOutput, calls=%fused_computation.19 | convolution fusion | flops 503316480 | bytes 3670016 | tf_op jit(solution)/shard_map/dot_general | solution.py:508
  58.7 0.0 copy-done.6
  58.7 0.0 copy-start.4
  58.7 0.9 fusion.9
  59.6 0.3 copy-done.4
  59.9 0.6 fusion.26
  60.5 0.7 copy-done.7
  61.1 1.7 fusion.1.refs_0_
  62.8 43.3 %shard_map.105 = bf16[32,2,8,1280]{3,2,1,0:T(8,128)(2,1)} custom-call(bf16[32,8,2560]{2,1,0:T(8,128)(2,1)} %fusion.1.refs_0_), custom_call_target="tpu_custom_call" | custom-call | bytes 40000000 | tf_op jit(solution)/shard_map/pallas_call | solution.py:324
  106.1 0.0 copy-start.8
  106.2 0.4 fusion.23
  106.6 0.3 copy-done.8
  107.0 0.2 fusion.40
  107.2 0.3 copy-done.3
  107.5 1.4 fusion.2
  108.8 21.0 %shard_map.106 = bf16[8,16,1280]{2,1,0:T(8,128)(2,1)} custom-call(bf16[8,16,1280]{2,1,0:T(8,128)(2,1)} %bitcast.75), custom_call_target="tpu_custom_call" | custom-call | bytes 40000000 | tf_op jit(solution)/shard_map/pallas_call | solution.py:119
  129.9 0.0 copy-start.9
  129.9 1.7 convert_reduce_fusion
  131.5 3.4 %shard_map.107 = f32[2,8,1280]{2,1,0:T(8,128)} custom-call(f32[2,8,1280]{2,1,0:T(8,128)} %bitcast.76), custom_call_target="tpu_custom_call" | custom-call | tf_op jit(solution)/shard_map/pallas_call | solution.py:358
  135.0 0.8 slice_bitcast_fusion.1
  135.8 0.1 fusion.32
  136.0 0.7 fusion.34.refs_0_
  136.7 26.5 %shard_map.108 = bf16[32,8,2560]{2,1,0:T(8,128)(2,1)} custom-call(bf16[8,2560]{1,0:T(8,128)(2,1)} %fusion.34.refs_0_), custom_call_target="tpu_custom_call" | custom-call | bytes 40000000 | tf_op jit(solution)/shard_map/pallas_call | solution.py:435
  163.2 0.1 constant_dynamic-slice_fusion
  163.3 0.1 eq.77
  163.4 0.0 all-gather.2.cloned.1.call-done
  163.4 6.4 %fusion.54 = (f32[256]{0:T(256)S(1)}, f32[256,1664]{1,0:T(8,128)S(1)}) fusion(bf16[2560,1664]{1,0:T(8,128)(2,1)} %all-gather.2.cloned.1.call-done, bf16[32,8,2560]{2,1,0:T(8,128)(2,1)} %shard_map.108), kind=kOutput, calls=%fused_computation.91 | convolution fusion | flops 2181463808 | bytes 11535360 | tf_op jit(solution)/shard_map/dot_general | solution.py:533
  169.9 0.8 exponential_reduce_fusion
  170.6 0.6 pad_maximum_fusion.refs_0_
  171.2 15.5 %shard_map.109 = f32[32,4,256]{2,1,0:T(4,128)} custom-call(f32[4,256]{1,0:T(4,128)} %pad_maximum_fusion.refs_0_), custom_call_target="tpu_custom_call" | custom-call | bytes 40000000 | tf_op jit(solution)/shard_map/pallas_call | solution.py:119
  186.7 1.3 fusion.53
  188.1 0.1 sub.70
  188.1 0.7 copy.36
  188.8 0.1 sub.72
  188.9 0.7 copy.37
  (27 shorter events, 0.3 us)
Async XLA Ops:
  7.2 99.0 %copy-start = (bf16[2560,64]{0,1:T(8,128)(2,1)S(1)}, bf16[2560,64]{0,1:T(8,128)(2,1)}, u32[]{:S(2)}) copy-start(bf16[2560,64]{0,1:T(8,128)(2,1)} %param.11) | copy-start | bytes 983044
  7.2 2.8 %copy-start.5 = (bf16[128,2560]{1,0:T(8,128)(2,1)S(1)}, bf16[128,2560]{1,0:T(8,128)(2,1)}, u32[]{:S(2)}) copy-start(bf16[128,2560]{1,0:T(8,128)(2,1)} %param.9) | copy-start | bytes 1966084
  7.2 156.2 %all-gather.2.cloned.1.call-start = ((), (), s32[]{:S(2)}) async-start(), calls=%async_computation | async-start | bytes 9052160 | tf_op jit(solution)/shard_map/all_gather | solution.py:467
  11.9 44.4 %copy-start.1 = (bf16[1,2560,384]{2,1,0:T(8,128)(2,1)S(1)}, bf16[1,2560,384]{2,1,0:T(8,128)(2,1)}, u32[]{:S(2)}) copy-start(bf16[1,2560,384]{2,1,0:T(8,128)(2,1)} %param.13) | copy-start | bytes 5898244
  56.3 2.4 %copy-start.2 = (bf16[32,8,2560]{2,1,0:T(8,128)(2,1)S(1)}, bf16[32,8,2560]{2,1,0:T(8,128)(2,1)}, u32[]{:S(2)}) copy-start(bf16[32,8,2560]{2,1,0:T(8,128)(2,1)} %get-tuple-element.5) | copy-start | bytes 3932164
  56.3 2.4 %copy-start.6 = (bf16[2560,384]{1,0:T(8,128)(2,1)S(1)}, bf16[2560,384]{1,0:T(8,128)(2,1)}, u32[]{:S(2)}) copy-start(bf16[2560,384]{1,0:T(8,128)(2,1)} %get-tuple-element.6) | copy-start | bytes 5898244
  58.7 1.2 copy-start.4
  59.9 1.2 copy-start.7
  106.1 0.7 copy-start.8
  106.2 1.3 copy-start.3
  107.5 27.5 %copy-start.10 = (bf16[2560]{0:T(1024)(128)(2,1)S(1)}, bf16[2560]{0:T(1024)(128)(2,1)}, u32[]{:S(2)}) copy-start(bf16[2560]{0:T(1024)(128)(2,1)} %param.15) | copy-start | bytes 15364
  129.9 33.3 %copy-start.9 = (s32[4096]{0:T(1024)S(1)}, s32[4096]{0:T(1024)}, u32[]{:S(2)}) copy-start(s32[4096]{0:T(1024)} %param.17) | copy-start | bytes 49156
Sparse Core Ops, SparseCore 0:
  10.1 61.4 all-gather.1

commit v3 on v1

--- a/solution.py
+++ b/solution.py
@@ -13,7 +13,6 @@
 NORM_EPSILON = 1e-06
 
 VMEM = pl.BlockSpec(memory_space=pltpu.VMEM)
-ANY = pl.BlockSpec(memory_space=pl.ANY)
 
 
 def rms_scale(values, gain_vector):
@@ -47,11 +46,9 @@
 
 def offsets(axis, count):
     if axis == "gy":
-        steps = [1]
-        for z in range(1, count // 4 + 1):
-            for sign in (1, -1):
-                if sign == 1 or 2 * z != count // 2:
-                    steps += [(sign * z, 0), (sign * z, 1)]
+        steps = []
+        for z in range(1, count // 2 + 1):
+            steps += [z] if 2 * z == count else [z, -z]
         return steps
     y_chips = count // X_CHIPS
     steps = []
@@ -67,14 +64,7 @@
 
 def partners(axis, count, me):
     if axis == "gy":
-        chips = count // 2
-        z, core = me // 2, lax.rem(me, 2)
-        found = [me + 1 - 2 * core]
-        for step in offsets(axis, count)[1:]:
-            found.append(
-                lax.rem(z + step[0] + chips, chips) * 2 + lax.rem(core + step[1], 2)
-            )
-        return found
+        return [lax.rem(me + step + count, count) for step in offsets(axis, count)]
     y_chips = count // X_CHIPS
     y, x = me // X_CHIPS, lax.rem(me, X_CHIPS)
     return [
@@ -86,15 +76,22 @@
 def exchange_kernel(axis, same, count, *refs):
     src, out, send_sem, recv_sem, own_sem = refs
     me = lax.axis_index(axis)
+    core = 0
+    if axis == "gy":
+        me, core = me // 2, lax.rem(me, 2)
+
+    def device(other):
+        return {axis: 2 * other + core if axis == "gy" else other}
+
     others = partners(axis, count, me)
-    greet([{axis: other} for other in others])
+    greet([device(other) for other in others])
     copies = [
         remote(
             src if same else src.at[other],
             out.at[me],
             send_sem.at[other],
             recv_sem.at[me],
-            {axis: other},
+            device(other),
         )
         for other in others
     ]
@@ -109,14 +106,14 @@
             out.at[other],
             send_sem.at[other],
             recv_sem.at[other],
-            {axis: other},
+            device(other),
         ).wait_recv()
     for copy in copies:
         copy.wait_send()
 
 
 def exchange(values, axis, collective_id, same=False):
-    count = lax.axis_size(axis)
+    count = lax.axis_size(axis) // (2 if axis == "gy" else 1)
     shape = (count,) + values.shape if same else values.shape
     return pl.pallas_call(
         functools.partial(exchange_kernel, axis, same, count),
@@ -135,62 +132,182 @@
     )(values)
 
 
-def dispatch_kernel(count, *refs):
-    (src, up, down, out, other_up, other_down, send_sem, recv_sem, own_sem, pair_sems) = refs
+def expert_kernel(count, *refs):
+    (src, up, down, out, rows, result, other_up, other_down) = refs[:8]
+    (send_sem, recv_sem, back_send, back_recv, own_sems, pair_sems) = refs[8:]
     me = lax.axis_index("gx")
     lane = lax.axis_index("gy")
-    others = partners("gx", count, me)
-    pair = {"gy": lane + 1 - 2 * lax.rem(lane, 2)}
-    greet([pair] + [{"gx": other} for other in others])
-    copies = [
-        remote(
-            src.at[other], out.at[me], send_sem.at[other], recv_sem.at[me], {"gx": other}
-        )
-        for other in others
+    core = lax.rem(lane, 2)
+    first = lane - core
+    pair = {"gy": first + 1 - core}
+    slots, width = src.shape[1:]
+    wide = width // 2
+    units = down.shape[0]
+    y_chips = count // X_CHIPS
+    steps = [(0, 0)] + [(dy % y_chips, dx) for dy, dx in offsets("gx", count)]
+    y, x = me // X_CHIPS, lax.rem(me, X_CHIPS)
+    peers = [
+        lax.rem(y + dy, y_chips) * X_CHIPS + lax.rem(x + dx, X_CHIPS) for dy, dx in steps
     ]
+    mirror = [
+        steps.index(((y_chips - dy) % y_chips, (X_CHIPS - dx) % X_CHIPS)) for dy, dx in steps
+    ]
+    greet([pair] + [{"gx": other, "gy": first + c} for other in peers[1:] for c in range(2)])
+
+    def half(c):
+        return pl.ds(pl.multiple_of(c * wide, 128), wide)
+
     swaps = [
         remote(up, other_up, pair_sems.at[0], pair_sems.at[1], pair),
         remote(down, other_down, pair_sems.at[2], pair_sems.at[3], pair),
     ]
-    for copy in copies:
-        copy.start()
     for copy in swaps:
         copy.start()
-    own = pltpu.make_async_copy(src.at[me], out.at[me], own_sem)
+    sent = [
+        remote(
+            src.at[peers[r]],
+            rows.at[mirror[r]],
+            send_sem.at[r],
+            recv_sem.at[mirror[r]],
+            {"gx": peers[r]},
+        )
+        for r in range(1, count)
+    ]
+    for copy in sent:
+        copy.start()
+    own = pltpu.make_async_copy(src.at[me], rows.at[0], own_sems.at[0])
     own.start()
     own.wait()
-    for other in others:
-        remote(
-            src.at[other], out.at[other], send_sem.at[other], recv_sem.at[other], {"gx": other}
-        ).wait_recv()
-    for copy in copies:
+    backs = []
+
+    def give_back(r):
+        for c in range(2):
+            if r:
+                copy = remote(
+                    result.at[r, :, half(c)],
+                    out.at[me, core],
+                    back_send.at[r, c],
+                    back_recv.at[mirror[r], core],
+                    {"gx": peers[r], "gy": first + c},
+                )
+                copy.start()
+                backs.append(copy)
+        if not r:
+            copy = remote(
+                result.at[0, :, half(1 - core)],
+                out.at[me, core],
+                back_send.at[0, 0],
+                back_recv.at[0, core],
+                pair,
+            )
+            copy.start()
+            backs.append(copy)
+            pltpu.make_async_copy(
+                result.at[0, :, half(core)], out.at[me, core], own_sems.at[1]
+            ).start()
+
+    def block(chunk, up_ref, down_ref):
+        lifted = jnp.dot(chunk, up_ref[...], preferred_element_type=jnp.float32)
+        gate = lifted[:, :units]
+        active = gate / (1.0 + jnp.exp(-gate)) * lifted[:, units:]
+        return jnp.dot(
+            active.astype(jnp.bfloat16), down_ref[...], preferred_element_type=jnp.float32
+        )
+
+    size = 8
+    for base in range(0, count, size):
+        for r in range(max(base, 1), base + size):
+            remote(
+                src.at[peers[r]], rows.at[r], send_sem.at[r], recv_sem.at[r], {"gx": peers[r]}
+            ).wait_recv()
+        if base:
+            for r in range(base - size, base):
+                give_back(r)
+        else:
+            for copy in swaps:
+                copy.wait_recv()
+        chunk = rows[pl.ds(base, size)].reshape(size * slots, width)
+        total = block(chunk, up, down) + block(chunk, other_up, other_down)
+        result[pl.ds(base, size)] = total.astype(jnp.bfloat16).reshape(size, slots, width)
+    for copy in sent + swaps:
         copy.wait_send()
-    for copy in swaps:
-        copy.wait()
-
-
-def dispatch_rows(values, up, down, collective_id):
+    for r in range(count - size, count):
+        give_back(r)
+    pltpu.make_async_copy(
+        result.at[0, :, half(core)], out.at[me, core], own_sems.at[1]
+    ).wait()
+    for r in range(1, count):
+        for c in range(2):
+            remote(
+                result.at[r, :, half(c)],
+                out.at[peers[r], c],
+                back_send.at[r, c],
+                back_recv.at[r, c],
+                {"gx": peers[r]},
+            ).wait_recv()
+    remote(
+        result.at[0, :, half(core)],
+        out.at[me, 1 - core],
+        back_send.at[0, 0],
+        back_recv.at[0, 1 - core],
+        pair,
+    ).wait_recv()
+    for copy in backs:
+        copy.wait_send()
+
+
+def through_experts(values, up, down, collective_id):
     count = lax.axis_size("gx")
+    slots, width = values.shape[1:]
     return pl.pallas_call(
-        functools.partial(dispatch_kernel, count),
-        out_shape=(
-            jax.ShapeDtypeStruct(values.shape, values.dtype),
-            jax.ShapeDtypeStruct(up.shape, up.dtype),
-            jax.ShapeDtypeStruct(down.shape, down.dtype),
-        ),
-        in_specs=[VMEM, ANY, ANY],
-        out_specs=(VMEM, ANY, ANY),
+        functools.partial(expert_kernel, count),
+        out_shape=jax.ShapeDtypeStruct((count, 2, slots, width // 2), values.dtype),
+        in_specs=[VMEM, VMEM, VMEM],
+        out_specs=VMEM,
         scratch_shapes=[
+            pltpu.VMEM(values.shape, values.dtype),
+            pltpu.VMEM(values.shape, values.dtype),
+            pltpu.VMEM(up.shape, up.dtype),
+            pltpu.VMEM(down.shape, down.dtype),
             pltpu.SemaphoreType.DMA((count,)),
             pltpu.SemaphoreType.DMA((count,)),
-            pltpu.SemaphoreType.DMA,
+            pltpu.SemaphoreType.DMA((count, 2)),
+            pltpu.SemaphoreType.DMA((count, 2)),
+            pltpu.SemaphoreType.DMA((2,)),
             pltpu.SemaphoreType.DMA((4,)),
         ],
-        compiler_params=pltpu.CompilerParams(collective_id=collective_id, has_side_effects=True),
+        compiler_params=pltpu.CompilerParams(
+            collective_id=collective_id, has_side_effects=True, vmem_limit_bytes=40 * 2**20
+        ),
         cost_estimate=pl.CostEstimate(
-            flops=0, bytes_accessed=100_000_000, transcendentals=0
+            flops=0, bytes_accessed=200_000_000, transcendentals=0
         ),
     )(values, up, down)
+
+
+def pair_kernel(src, out, send_sem, recv_sem, own_sem):
+    lane = lax.axis_index("gy")
+    core = lax.rem(lane, 2)
+    pair = {"gy": lane + 1 - 2 * core}
+    greet([pair])
+    copy = remote(src.at[1 - core], out.at[core], send_sem, recv_sem, pair)
+    copy.start()
+    own = pltpu.make_async_copy(src.at[core], out.at[core], own_sem)
+    own.start()
+    own.wait()
+    copy.wait_send()
+    remote(src.at[core], out.at[1 - core], send_sem, recv_sem, pair).wait_recv()
+
+
+def pair_swap(values, collective_id):
+    return pl.pallas_call(
+        pair_kernel,
+        out_shape=jax.ShapeDtypeStruct(values.shape, values.dtype),
+        in_specs=[VMEM],
+        out_specs=VMEM,
+        scratch_shapes=[pltpu.SemaphoreType.DMA] * 3,
+        compiler_params=pltpu.CompilerParams(collective_id=collective_id, has_side_effects=True),
+    )(values)
 
 
 def relay_kernel(count, *refs):
@@ -203,8 +320,8 @@
         return lax.rem(row + y_chips, y_chips) * X_CHIPS + lax.rem(column, X_CHIPS)
 
     above, below = at(y + 1, x), at(y - 1, x)
-    sides = [at(y, x + 1), at(y, x + 3), at(y, x + 2)]
-    greet([{"gx": other} for other in [above, below] + sides])
+    right, left = at(y, x + 1), at(y, x + 3)
+    greet([{"gx": other} for other in (above, below, right, left)])
     sent = []
 
     def send(block, source, target):
@@ -219,30 +336,40 @@
             src, out.at[block], send_sem.at[0], recv_sem.at[block], {"gx": above}
         ).wait_recv()
 
+    def across(k):
+        near, far = (x + 3, right) if k % 2 == 0 else (x + 1, left)
+        block = at(y + k, near)
+        arrived(block)
+        send(block, out.at[block], far)
+
     send(me, src, above)
     send(me, src, below)
-    for side in sides:
-        send(me, src, side)
+    send(me, src, right)
+    send(me, src, left)
     own = pltpu.make_async_copy(src, out.at[me], own_sem)
     own.start()
     half = y_chips // 2
+    order = [0]
     for step in range(1, half + 1):
-        block = at(y - step, x)
-        arrived(block)
+        order.append(y_chips - step)
         if step < half:
-            send(block, out.at[block], above)
-        for side in sides:
-            send(block, out.at[block], side)
-        if step < half:
-            block = at(y + step, x)
+            order.append(step)
+    for i, k in enumerate(order):
+        if k:
+            block = at(y + k, x)
             arrived(block)
-            if step < half - 1:
+            if half < k:
+                send(block, out.at[block], above)
+            elif k < half - 1:
                 send(block, out.at[block], below)
-            for side in sides:
-                send(block, out.at[block], side)
-    for row in range(y_chips):
-        for column in range(1, X_CHIPS):
-            arrived(at(y + row, x + column))
+            send(block, out.at[block], right)
+            send(block, out.at[block], left)
+        if i >= 1:
+            across(order[i - 1])
+    across(order[-1])
+    for k in order:
+        arrived(at(y + k, x + (1 if k % 2 == 0 else 3)))
+        arrived(at(y + k, x + 2))
     own.wait()
     for copy in sent:
         copy.wait_send()
@@ -277,8 +404,8 @@
     group_index = lax.axis_index("gx")
     lane_index = lax.axis_index("gy")
     expert_count = router_weight.shape[1]
-    unit_count = w_down.shape[1]
-    slot_count = tok_rows // 16
+    slot_count = tok_rows // 8
+    half_slots = slot_count // 2
     share_rows = tok_rows // lane_count
     columns = head_weight.shape[1]
     head_full = lax.all_gather(head_weight, "gy", axis=0, tiled=True)
@@ -290,9 +417,8 @@
     gate_table = jnp.sum(jnp.where(chosen, gate_values.astype(jnp.float32)[:, :, None], 0.0), 1)
     member = jnp.sum(chosen.astype(jnp.int32), 1)
     slot_rank = jnp.cumsum(member, 0) - member
-    slot_base = lax.rem(lane_index, 2) * slot_count
     slot_hit = (member[:, :, None] == 1) & (
-        slot_rank[:, :, None] == slot_base + jnp.arange(slot_count, dtype=jnp.int32)[None, None, :]
+        slot_rank[:, :, None] == jnp.arange(slot_count, dtype=jnp.int32)[None, None, :]
     )
     owner_expert = (
         jnp.arange(group_count, dtype=jnp.int32) * lane_count + lane_index
@@ -306,8 +432,10 @@
         slot_hit.astype(jnp.bfloat16),
         preferred_element_type=jnp.float32,
     ).astype(jnp.bfloat16)
+    core = lax.rem(lane_index, 2)
+    own_slots = lax.dynamic_slice_in_dim(dispatch, core * half_slots, half_slots, 1)
     outgoing = jnp.einsum(
-        "tcn,nd->tcd", dispatch, normed, preferred_element_type=jnp.float32
+        "tcn,nd->tcd", own_slots, normed, preferred_element_type=jnp.float32
     ).astype(jnp.bfloat16)
     expert_gate = jnp.einsum(
         "te,ne->tn",
@@ -316,24 +444,19 @@
         preferred_element_type=jnp.float32,
     )
     combine = (dispatch.astype(jnp.float32) * expert_gate[:, None, :]).astype(jnp.bfloat16)
-    own_up, own_down = w_gate_up[0], w_down[0]
-    rows, pair_up, pair_down = dispatch_rows(outgoing, own_up, own_down, 1)
-    rows = rows.reshape(group_count * slot_count, width)
-
-    def block(up, down):
-        lifted = jnp.dot(rows, up, preferred_element_type=jnp.float32)
-        active = (
-            jax.nn.silu(lifted[:, :unit_count]) * lifted[:, unit_count:]
-        ).astype(jnp.bfloat16)
-        return jnp.dot(active, down, preferred_element_type=jnp.float32)
-
-    result = (block(own_up, own_down) + block(pair_up, pair_down)).astype(jnp.bfloat16)
-    returned = exchange(result.reshape(group_count, slot_count, width), "gx", 2)
+    returned = through_experts(outgoing, w_gate_up[0], w_down[0], 1)
     partial_value = jnp.einsum(
-        "tcn,tcd->nd", combine, returned, preferred_element_type=jnp.float32
+        "tcn,tcd->nd",
+        combine,
+        returned.reshape(group_count, slot_count, width // 2),
+        preferred_element_type=jnp.float32,
     ).astype(jnp.bfloat16)
-    pieces = exchange(partial_value.reshape(lane_count, share_rows, width), "gy", 3)
-    summed = jnp.sum(pieces.astype(jnp.float32), 0)
+    chips = lane_count // 2
+    pieces = exchange(partial_value.reshape(chips, 2 * share_rows, width // 2), "gy", 3)
+    halves = pair_swap(
+        jnp.sum(pieces.astype(jnp.float32), 0).reshape(2, share_rows, width // 2), 6
+    )
+    summed = jnp.concatenate([halves[0], halves[1]], axis=-1)
     residual = lax.dynamic_slice_in_dim(hidden_in, lane_index * share_rows, share_rows, 0)
     layer_out = (residual.astype(jnp.float32) + summed).astype(jnp.bfloat16)
     final_states = rms_scale(layer_out, final_gain).astype(jnp.bfloat16)

time: 188 us -> 172 us (0.915)
  Pallas kernels: 147 us -> 135 us
  matrix products: 15.9 us -> 10.5 us
    pallas_call x3 -> x2, Pallas kernels: 81.9 us -> 34 us  [exchange(): pl.pallas_call(functools.partial(exchange_kernel, axis, same, count), out...]
    pallas_call x1 -> x2, Pallas kernels: 38.9 us -> 72 us  [the longest x1 68.6 us: through_experts(): pl.pallas_call(functools.partial(expert_kernel, count), out_shape=jax.Sha...]
    dot_general x6 -> x2, matrix products: 8.59 us -> 3.21 us  [the longest x1 1.85 us: shards(): jnp.einsum('tcn,nd->tcd', own_slots, normed, preferred_element_type=jnp.f...]
    pallas_call x1, Pallas kernels: 25.8 us -> 29.4 us  [relay_gather(): pl.pallas_call(functools.partial(relay_kernel, count), out_shape=jax.Shap...]
  transfers between devices with their start and end apart: 1 -> 1, of which waited for: 0 -> 0; matrix products, arithmetic and copies ran while one was open for 7% -> 6% of each run, Pallas kernels for 71% -> 71%
where the time goes in v3:
time: 172 us
  Pallas kernels  135 us (78%)
  between operations  14.3 us (8%)
  matrix products  10.5 us (6%)
  other arithmetic  7.95 us (5%)
  local copies, waits for them, and re-layouts  2.69 us (2%)
    pallas_call x1, Pallas kernels, through_experts(): pl.pallas_call(functools.partial(expert_kernel, count), out_shape=jax.Sha...  68.6 us
    pallas_call x2, Pallas kernels, exchange(): pl.pallas_call(functools.partial(exchange_kernel, axis, same, count), out...  34 us
    pallas_call x1, Pallas kernels, relay_gather(): pl.pallas_call(functools.partial(relay_kernel, count), out_shape=jax.Shap...  29.4 us
    dot_general x1, matrix products, shards(): logits = jnp.dot(gathered, head_full, preferred_element_type=jnp.float32)  6.45 us
    pallas_call x1, Pallas kernels, pair_swap(): pl.pallas_call(pair_kernel, out_shape=jax.ShapeDtypeStruct(values.shape,...  3.44 us
  transfers between devices with their start and end apart: 1, of which 0 were waited for; matrix products, arithmetic and copies ran while one was open for 6% of the time, Pallas kernels for 71%

profile of v3, /device:TPU:64, one launch (start us, length us, event | category | flops | bytes accessed | tf_op | source)
XLA Modules:
  0.0 171.6 jit_solution(8327344581985300873)
XLA Ops:
  7.2 0.0 copy-start
  7.2 0.0 copy-start.3
  7.2 0.0 all-gather.2.cloned.1.call-start
  7.2 0.7 all-gather.2.cloned.1.call-update
  7.9 0.7 convert_reduce_fusion.1
  8.7 0.0 copy-start.4
  8.7 0.1 copy.29
  8.8 0.2 reduce_window_sum.11
  8.9 0.1 copy.31
  9.0 0.7 convert_element_type.74
  9.7 0.0 copy-done.3
  9.7 0.2 fusion.2
  10.0 0.0 copy-done
  10.0 0.0 copy-start.2
  10.0 0.4 fusion.15
  10.4 0.0 copy-done.4
  10.4 0.0 copy-start.1
  10.5 0.2 convolution_convert_fusion.1
  10.8 1.9 %convolution_convert_fusion.refs_0_ = bf16[32,8,2560]{2,1,0:T(8,128)(2,1)S(1)} fusion(bf16[128,2560]{1,0:T(8,128)(2,1)} %param.9, f32[2560]{0:T(1024)S(1)} %convert_element_type.74, f32[128]{0:T(128)S(1)} %add_rsqrt_fusion.1, bf16[32,8,128]{2,0,1:T(8,128)(2,1)S(1)} %dynamic-slice_bitcast_fusion), kind=kOutput, calls=%fused_computation | convolution fusion | flops 169738240 | bytes 2042368 | tf_op jit(solution)/shard_map/tcn,nd->tcd/dot_general | solution.py:437
  12.6 0.0 copy-done.2
  12.6 0.0 copy-done.1
  12.6 68.6 %shard_map.104 = bf16[32,2,8,1280]{3,2,1,0:T(8,128)(2,1)S(1)} custom-call(bf16[32,8,2560]{2,1,0:T(8,128)(2,1)S(1)} %convolution_convert_fusion.refs_0_, bf16[2560,384]{1,0:T(8,128)(2,1)S(1)} %bitcast.60, bf16[192,2560]{1,0:T(8,128)(2,1)S(1)} %bitcast.61), custom_call_target="tpu_custom_call" | custom-call | bytes 200000000 | tf_op jit(solution)/shard_map/pallas_call | solution.py:262
  81.3 0.2 fusion.27
  81.5 0.0 copy-start.6
  81.5 1.4 fusion
  82.9 19.9 %shard_map.105 = bf16[8,16,1280]{2,1,0:T(8,128)(2,1)} custom-call(bf16[8,16,1280]{2,1,0:T(8,128)(2,1)} %bitcast.62), custom_call_target="tpu_custom_call" | custom-call | bytes 40000000 | tf_op jit(solution)/shard_map/pallas_call | solution.py:118
  102.7 0.0 copy-start.5
  102.7 1.7 convert_reduce_fusion
  104.4 3.4 %shard_map.106 = f32[2,8,1280]{2,1,0:T(8,128)} custom-call(f32[2,8,1280]{2,1,0:T(8,128)} %bitcast.63), custom_call_target="tpu_custom_call" | custom-call | tf_op jit(solution)/shard_map/pallas_call | solution.py:303
  107.8 0.0 copy-done.6
  107.9 0.8 slice_bitcast_fusion.1
  108.7 0.9 fusion.19
  109.6 0.7 fusion.21.refs_0_
  110.3 29.4 %shard_map.107 = bf16[32,8,2560]{2,1,0:T(8,128)(2,1)} custom-call(bf16[8,2560]{1,0:T(8,128)(2,1)} %fusion.21.refs_0_), custom_call_target="tpu_custom_call" | custom-call | bytes 40000000 | tf_op jit(solution)/shard_map/pallas_call | solution.py:380
  139.7 0.0 copy-done.5
  139.7 0.1 constant_dynamic-slice_fusion
  139.8 0.1 eq.77
  139.9 0.0 all-gather.2.cloned.1.call-done
  139.9 6.4 %fusion.37 = (f32[256]{0:T(256)S(1)}, f32[256,1664]{1,0:T(8,128)S(1)}) fusion(bf16[2560,1664]{1,0:T(8,128)(2,1)} %all-gather.2.cloned.1.call-done, bf16[32,8,2560]{2,1,0:T(8,128)(2,1)} %shard_map.107), kind=kOutput, calls=%fused_computation.73 | convolution fusion | flops 2181463808 | bytes 11535360 | tf_op jit(solution)/shard_map/dot_general | solution.py:465
  146.4 0.8 exponential_reduce_fusion
  147.1 0.6 pad_maximum_fusion.refs_0_
  147.8 14.1 %shard_map.108 = f32[32,4,256]{2,1,0:T(4,128)} custom-call(f32[4,256]{1,0:T(4,128)} %pad_maximum_fusion.refs_0_), custom_call_target="tpu_custom_call" | custom-call | bytes 40000000 | tf_op jit(solution)/shard_map/pallas_call | solution.py:118
  161.9 1.3 fusion.36
  163.2 0.1 sub.70
  163.3 0.7 copy.36
  164.0 0.1 sub.72
  164.1 0.7 copy.37
  (15 shorter events, 0.2 us)
Async XLA Ops:
  7.2 2.8 %copy-start = (bf16[2560,64]{0,1:T(8,128)(2,1)S(1)}, bf16[2560,64]{0,1:T(8,128)(2,1)}, u32[]{:S(2)}) copy-start(bf16[2560,64]{0,1:T(8,128)(2,1)} %param.11) | copy-start | bytes 983044
  7.2 2.6 %copy-start.3 = (bf16[128,2560]{1,0:T(8,128)(2,1)S(1)}, bf16[128,2560]{1,0:T(8,128)(2,1)}, u32[]{:S(2)}) copy-start(bf16[128,2560]{1,0:T(8,128)(2,1)} %param.9) | copy-start | bytes 1966084
  7.2 132.7 %all-gather.2.cloned.1.call-start = ((), (), s32[]{:S(2)}) async-start(), calls=%async_computation | async-start | bytes 9052160 | tf_op jit(solution)/shard_map/all_gather | solution.py:411
  8.7 1.7 %copy-start.4 = (s32[128,6]{0,1:T(8,128)S(1)}, s32[128,6]{0,1:T(8,128)}, u32[]{:S(2)}) copy-start(s32[128,6]{0,1:T(8,128)} %param.12) | copy-start | bytes 9220
  10.0 2.7 %copy-start.2 = (bf16[1,192,2560]{2,1,0:T(8,128)(2,1)S(1)}, bf16[1,192,2560]{2,1,0:T(8,128)(2,1)}, u32[]{:S(2)}) copy-start(bf16[1,192,2560]{2,1,0:T(8,128)(2,1)} %param.14) | copy-start | bytes 2949124
  10.4 2.2 %copy-start.1 = (bf16[1,2560,384]{2,1,0:T(8,128)(2,1)S(1)}, bf16[1,2560,384]{2,1,0:T(8,128)(2,1)}, u32[]{:S(2)}) copy-start(bf16[1,2560,384]{2,1,0:T(8,128)(2,1)} %param.13) | copy-start | bytes 5898244
  81.5 26.4 %copy-start.6 = (bf16[2560]{0:T(1024)(128)(2,1)S(1)}, bf16[2560]{0:T(1024)(128)(2,1)}, u32[]{:S(2)}) copy-start(bf16[2560]{0:T(1024)(128)(2,1)} %param.15) | copy-start | bytes 15364
  102.7 37.0 %copy-start.5 = (s32[4096]{0:T(1024)S(1)}, s32[4096]{0:T(1024)}, u32[]{:S(2)}) copy-start(s32[4096]{0:T(1024)} %param.17) | copy-start | bytes 49156
Sparse Core Ops, SparseCore 0:
  10.1 61.4 all-gather.1

commit v4 on v3

--- a/solution.py
+++ b/solution.py
@@ -134,12 +134,15 @@
 
 def expert_kernel(count, *refs):
     (src, up, down, out, rows, result, other_up, other_down) = refs[:8]
-    (send_sem, recv_sem, back_send, back_recv, own_sems, pair_sems) = refs[8:]
+    (send_sem, recv_sem, back_send, back_recv, own_sems, pair_sems) = refs[8:14]
+    (hand_send, hand_recv) = refs[14:]
     me = lax.axis_index("gx")
     lane = lax.axis_index("gy")
     core = lax.rem(lane, 2)
     first = lane - core
     pair = {"gy": first + 1 - core}
+    side = lax.rem(lane // 2, 2)
+    next_chip = {"gy": lane + 2 - 4 * side}
     slots, width = src.shape[1:]
     wide = width // 2
     units = down.shape[0]
@@ -152,7 +155,10 @@
     mirror = [
         steps.index(((y_chips - dy) % y_chips, (X_CHIPS - dx) % X_CHIPS)) for dy, dx in steps
     ]
-    greet([pair] + [{"gx": other, "gy": first + c} for other in peers[1:] for c in range(2)])
+    greet(
+        [pair, next_chip]
+        + [{"gx": other, "gy": first + c} for other in peers[1:] for c in range(2)]
+    )
 
     def half(c):
         return pl.ds(pl.multiple_of(c * wide, 128), wide)
@@ -165,8 +171,8 @@
         copy.start()
     sent = [
         remote(
-            src.at[peers[r]],
-            rows.at[mirror[r]],
+            src.at[peers[r], :, half(side)],
+            rows.at[mirror[r], :, half(side)],
             send_sem.at[r],
             recv_sem.at[mirror[r]],
             {"gx": peers[r]},
@@ -215,21 +221,43 @@
         )
 
     size = 8
+    hands = []
     for base in range(0, count, size):
         for r in range(max(base, 1), base + size):
             remote(
-                src.at[peers[r]], rows.at[r], send_sem.at[r], recv_sem.at[r], {"gx": peers[r]}
+                src.at[peers[r], :, half(side)],
+                rows.at[r, :, half(side)],
+                send_sem.at[r],
+                recv_sem.at[r],
+                {"gx": peers[r]},
             ).wait_recv()
+            hand = remote(
+                rows.at[r, :, half(side)],
+                rows.at[r, :, half(side)],
+                hand_send.at[r],
+                hand_recv.at[r],
+                next_chip,
+            )
+            hand.start()
+            hands.append(hand)
         if base:
             for r in range(base - size, base):
                 give_back(r)
         else:
             for copy in swaps:
                 copy.wait_recv()
+        for r in range(max(base, 1), base + size):
+            remote(
+                rows.at[r, :, half(side)],
+                rows.at[r, :, half(1 - side)],
+                hand_send.at[r],
+                hand_recv.at[r],
+                next_chip,
+            ).wait_recv()
         chunk = rows[pl.ds(base, size)].reshape(size * slots, width)
         total = block(chunk, up, down) + block(chunk, other_up, other_down)
         result[pl.ds(base, size)] = total.astype(jnp.bfloat16).reshape(size, slots, width)
-    for copy in sent + swaps:
+    for copy in sent + swaps + hands:
         copy.wait_send()
     for r in range(count - size, count):
         give_back(r)
@@ -275,6 +303,8 @@
             pltpu.SemaphoreType.DMA((count, 2)),
             pltpu.SemaphoreType.DMA((2,)),
             pltpu.SemaphoreType.DMA((4,)),
+            pltpu.SemaphoreType.DMA((count,)),
+            pltpu.SemaphoreType.DMA((count,)),
         ],
         compiler_params=pltpu.CompilerParams(
             collective_id=collective_id, has_side_effects=True, vmem_limit_bytes=40 * 2**20

time: 172 us -> 170 us (0.988)
  the two profiles are of different devices: /device:TPU:64 before, /device:TPU:2 now
where the time goes in v4:
time: 170 us; the launch traced here: 169 us
  Pallas kernels  133 us (78%)
  between operations  14.3 us (8%)
  matrix products  10.5 us (6%)
  other arithmetic  7.95 us (5%)
  local copies, waits for them, and re-layouts  2.69 us (2%)
    pallas_call x1, Pallas kernels, through_experts(): pl.pallas_call(functools.partial(expert_kernel, count), out_shape=jax.Sha...  66 us
    pallas_call x2, Pallas kernels, exchange(): pl.pallas_call(functools.partial(exchange_kernel, axis, same, count), out...  35.5 us
    pallas_call x1, Pallas kernels, relay_gather(): pl.pallas_call(functools.partial(relay_kernel, count), out_shape=jax.Shap...  27.8 us
    dot_general x1, matrix products, shards(): logits = jnp.dot(gathered, head_full, preferred_element_type=jnp.float32)  6.45 us
    pallas_call x1, Pallas kernels, pair_swap(): pl.pallas_call(pair_kernel, out_shape=jax.ShapeDtypeStruct(values.shape,...  3.44 us
  transfers between devices with their start and end apart: 1, of which 0 were waited for; matrix products, arithmetic and copies ran while one was open for 6% of the time, Pallas kernels for 70%

profile of v4, /device:TPU:2, one launch (start us, length us, event | category | flops | bytes accessed | tf_op | source)
XLA Modules:
  0.0 168.9 jit_solution(13936537988998407472)
XLA Ops:
  7.2 0.0 copy-start
  7.2 0.0 copy-start.3
  7.2 0.0 all-gather.2.cloned.1.call-start
  7.2 0.7 all-gather.2.cloned.1.call-update
  7.9 0.7 convert_reduce_fusion.1
  8.7 0.0 copy-start.4
  8.7 0.1 copy.29
  8.8 0.2 reduce_window_sum.11
  8.9 0.1 copy.31
  9.0 0.7 convert_element_type.74
  9.7 0.0 copy-done.3
  9.7 0.2 fusion.2
  10.0 0.0 copy-done
  10.0 0.0 copy-start.2
  10.0 0.4 fusion.15
  10.4 0.0 copy-done.4
  10.4 0.0 copy-start.1
  10.5 0.2 convolution_convert_fusion.1
  10.8 1.9 %convolution_convert_fusion.refs_0_ = bf16[32,8,2560]{2,1,0:T(8,128)(2,1)S(1)} fusion(bf16[128,2560]{1,0:T(8,128)(2,1)} %param.9, f32[2560]{0:T(1024)S(1)} %convert_element_type.74, f32[128]{0:T(128)S(1)} %add_rsqrt_fusion.1, bf16[32,8,128]{2,0,1:T(8,128)(2,1)S(1)} %dynamic-slice_bitcast_fusion), kind=kOutput, calls=%fused_computation | convolution fusion | flops 169738240 | bytes 2042368 | tf_op jit(solution)/shard_map/tcn,nd->tcd/dot_general | solution.py:467
  12.6 0.0 copy-done.2
  12.6 0.0 copy-done.1
  12.6 66.0 %shard_map.104 = bf16[32,2,8,1280]{3,2,1,0:T(8,128)(2,1)S(1)} custom-call(bf16[32,8,2560]{2,1,0:T(8,128)(2,1)S(1)} %convolution_convert_fusion.refs_0_, bf16[2560,384]{1,0:T(8,128)(2,1)S(1)} %bitcast.60, bf16[192,2560]{1,0:T(8,128)(2,1)S(1)} %bitcast.61), custom_call_target="tpu_custom_call" | custom-call | bytes 200000000 | tf_op jit(solution)/shard_map/pallas_call | solution.py:290
  78.7 0.2 fusion.27
  78.9 0.0 copy-start.6
  78.9 1.4 fusion
  80.2 20.2 %shard_map.105 = bf16[8,16,1280]{2,1,0:T(8,128)(2,1)} custom-call(bf16[8,16,1280]{2,1,0:T(8,128)(2,1)} %bitcast.62), custom_call_target="tpu_custom_call" | custom-call | bytes 40000000 | tf_op jit(solution)/shard_map/pallas_call | solution.py:118
  100.4 0.0 copy-start.5
  100.4 1.7 convert_reduce_fusion
  102.1 3.4 %shard_map.106 = f32[2,8,1280]{2,1,0:T(8,128)} custom-call(f32[2,8,1280]{2,1,0:T(8,128)} %bitcast.63), custom_call_target="tpu_custom_call" | custom-call | tf_op jit(solution)/shard_map/pallas_call | solution.py:333
  105.5 0.0 copy-done.6
  105.6 0.8 slice_bitcast_fusion.1
  106.4 0.9 fusion.19
  107.3 0.7 fusion.21.refs_0_
  108.0 27.8 %shard_map.107 = bf16[32,8,2560]{2,1,0:T(8,128)(2,1)} custom-call(bf16[8,2560]{1,0:T(8,128)(2,1)} %fusion.21.refs_0_), custom_call_target="tpu_custom_call" | custom-call | bytes 40000000 | tf_op jit(solution)/shard_map/pallas_call | solution.py:410
  135.8 0.0 copy-done.5
  135.8 0.1 constant_dynamic-slice_fusion
  135.9 0.1 eq.77
  136.0 0.0 all-gather.2.cloned.1.call-done
  136.0 6.4 %fusion.37 = (f32[256]{0:T(256)S(1)}, f32[256,1664]{1,0:T(8,128)S(1)}) fusion(bf16[2560,1664]{1,0:T(8,128)(2,1)} %all-gather.2.cloned.1.call-done, bf16[32,8,2560]{2,1,0:T(8,128)(2,1)} %shard_map.107), kind=kOutput, calls=%fused_computation.73 | convolution fusion | flops 2181463808 | bytes 11535360 | tf_op jit(solution)/shard_map/dot_general | solution.py:495
  142.5 0.8 exponential_reduce_fusion
  143.3 0.6 pad_maximum_fusion.refs_0_
  143.9 15.3 %shard_map.108 = f32[32,4,256]{2,1,0:T(4,128)} custom-call(f32[4,256]{1,0:T(4,128)} %pad_maximum_fusion.refs_0_), custom_call_target="tpu_custom_call" | custom-call | bytes 40000000 | tf_op jit(solution)/shard_map/pallas_call | solution.py:118
  159.2 1.3 fusion.36
  160.5 0.1 sub.70
  160.6 0.7 copy.36
  161.3 0.1 sub.72
  161.4 0.7 copy.37
  (15 shorter events, 0.2 us)
Async XLA Ops:
  7.2 2.8 %copy-start = (bf16[2560,64]{0,1:T(8,128)(2,1)S(1)}, bf16[2560,64]{0,1:T(8,128)(2,1)}, u32[]{:S(2)}) copy-start(bf16[2560,64]{0,1:T(8,128)(2,1)} %param.11) | copy-start | bytes 983044
  7.2 2.6 %copy-start.3 = (bf16[128,2560]{1,0:T(8,128)(2,1)S(1)}, bf16[128,2560]{1,0:T(8,128)(2,1)}, u32[]{:S(2)}) copy-start(bf16[128,2560]{1,0:T(8,128)(2,1)} %param.9) | copy-start | bytes 1966084
  7.2 128.8 %all-gather.2.cloned.1.call-start = ((), (), s32[]{:S(2)}) async-start(), calls=%async_computation | async-start | bytes 9052160 | tf_op jit(solution)/shard_map/all_gather | solution.py:441
  8.7 1.7 %copy-start.4 = (s32[128,6]{0,1:T(8,128)S(1)}, s32[128,6]{0,1:T(8,128)}, u32[]{:S(2)}) copy-start(s32[128,6]{0,1:T(8,128)} %param.12) | copy-start | bytes 9220
  10.0 2.7 %copy-start.2 = (bf16[1,192,2560]{2,1,0:T(8,128)(2,1)S(1)}, bf16[1,192,2560]{2,1,0:T(8,128)(2,1)}, u32[]{:S(2)}) copy-start(bf16[1,192,2560]{2,1,0:T(8,128)(2,1)} %param.14) | copy-start | bytes 2949124
  10.4 2.2 %copy-start.1 = (bf16[1,2560,384]{2,1,0:T(8,128)(2,1)S(1)}, bf16[1,2560,384]{2,1,0:T(8,128)(2,1)}, u32[]{:S(2)}) copy-start(bf16[1,2560,384]{2,1,0:T(8,128)(2,1)} %param.13) | copy-start | bytes 5898244
  78.9 26.7 %copy-start.6 = (bf16[2560]{0:T(1024)(128)(2,1)S(1)}, bf16[2560]{0:T(1024)(128)(2,1)}, u32[]{:S(2)}) copy-start(bf16[2560]{0:T(1024)(128)(2,1)} %param.15) | copy-start | bytes 15364
  100.4 35.4 %copy-start.5 = (s32[4096]{0:T(1024)S(1)}, s32[4096]{0:T(1024)}, u32[]{:S(2)}) copy-start(s32[4096]{0:T(1024)} %param.17) | copy-start | bytes 49156
Sparse Core Ops, SparseCore 0:
  10.1 76.2 all-gather.1

commit v5 on v4

--- a/solution.py
+++ b/solution.py
@@ -222,7 +222,8 @@
 
     size = 8
     hands = []
-    for base in range(0, count, size):
+
+    def hand_on(base):
         for r in range(max(base, 1), base + size):
             remote(
                 src.at[peers[r], :, half(side)],
@@ -240,12 +241,16 @@
             )
             hand.start()
             hands.append(hand)
+
+    hand_on(0)
+    for copy in swaps:
+        copy.wait_recv()
+    for base in range(0, count, size):
+        if base + size < count:
+            hand_on(base + size)
         if base:
             for r in range(base - size, base):
                 give_back(r)
-        else:
-            for copy in swaps:
-                copy.wait_recv()
         for r in range(max(base, 1), base + size):
             remote(
                 rows.at[r, :, half(side)],
@@ -350,8 +355,9 @@
         return lax.rem(row + y_chips, y_chips) * X_CHIPS + lax.rem(column, X_CHIPS)
 
     above, below = at(y + 1, x), at(y - 1, x)
+    above2, below2 = at(y + 2, x), at(y - 2, x)
     right, left = at(y, x + 1), at(y, x + 3)
-    greet([{"gx": other} for other in (above, below, right, left)])
+    greet([{"gx": other} for other in (above, below, above2, below2, right, left)])
     sent = []
 
     def send(block, source, target):
@@ -374,10 +380,13 @@
 
     send(me, src, above)
     send(me, src, below)
+    send(me, src, above2)
+    send(me, src, below2)
     send(me, src, right)
     send(me, src, left)
     own = pltpu.make_async_copy(src, out.at[me], own_sem)
     own.start()
+    assert y_chips == 8
     half = y_chips // 2
     order = [0]
     for step in range(1, half + 1):
@@ -388,9 +397,10 @@
         if k:
             block = at(y + k, x)
             arrived(block)
-            if half < k:
+            if k == y_chips - 2:
+                send(block, out.at[block], above2)
                 send(block, out.at[block], above)
-            elif k < half - 1:
+            elif k == 2:
                 send(block, out.at[block], below)
             send(block, out.at[block], right)
             send(block, out.at[block], left)

time: 170 us -> 165 us (0.971)
  the two profiles are of different devices: /device:TPU:2 before, /device:TPU:64 now
where the time goes in v5:
time: 165 us
  Pallas kernels  129 us (78%)
  between operations  14.3 us (9%)
  matrix products  10.5 us (6%)
  other arithmetic  7.95 us (5%)
  local copies, waits for them, and re-layouts  2.69 us (2%)
    pallas_call x1, Pallas kernels, through_experts(): pl.pallas_call(functools.partial(expert_kernel, count), out_shape=jax.Sha...  58.5 us
    pallas_call x2, Pallas kernels, exchange(): pl.pallas_call(functools.partial(exchange_kernel, axis, same, count), out...  35.7 us
    pallas_call x1, Pallas kernels, relay_gather(): pl.pallas_call(functools.partial(relay_kernel, count), out_shape=jax.Shap...  30.9 us
    dot_general x1, matrix products, shards(): logits = jnp.dot(gathered, head_full, preferred_element_type=jnp.float32)  6.45 us
    pallas_call x1, Pallas kernels, pair_swap(): pl.pallas_call(pair_kernel, out_shape=jax.ShapeDtypeStruct(values.shape,...  3.44 us
  transfers between devices with their start and end apart: 1, of which 0 were waited for; matrix products, arithmetic and copies ran while one was open for 6% of the time, Pallas kernels for 70%

profile of v5, /device:TPU:64, one launch (start us, length us, event | category | flops | bytes accessed | tf_op | source)
XLA Modules:
  0.0 164.7 jit_solution(8599255330902544336)
XLA Ops:
  7.2 0.0 copy-start
  7.2 0.0 copy-start.3
  7.2 0.0 all-gather.2.cloned.1.call-start
  7.2 0.7 all-gather.2.cloned.1.call-update
  7.9 0.7 convert_reduce_fusion.1
  8.7 0.0 copy-start.4
  8.7 0.1 copy.29
  8.8 0.2 reduce_window_sum.11
  8.9 0.1 copy.31
  9.0 0.7 convert_element_type.74
  9.7 0.0 copy-done.3
  9.7 0.2 fusion.2
  10.0 0.0 copy-done
  10.0 0.0 copy-start.2
  10.0 0.4 fusion.15
  10.4 0.0 copy-done.4
  10.4 0.0 copy-start.1
  10.5 0.2 convolution_convert_fusion.1
  10.8 1.9 %convolution_convert_fusion.refs_0_ = bf16[32,8,2560]{2,1,0:T(8,128)(2,1)S(1)} fusion(bf16[128,2560]{1,0:T(8,128)(2,1)} %param.9, f32[2560]{0:T(1024)S(1)} %convert_element_type.74, f32[128]{0:T(128)S(1)} %add_rsqrt_fusion.1, bf16[32,8,128]{2,0,1:T(8,128)(2,1)S(1)} %dynamic-slice_bitcast_fusion), kind=kOutput, calls=%fused_computation | convolution fusion | flops 169738240 | bytes 2042368 | tf_op jit(solution)/shard_map/tcn,nd->tcd/dot_general | solution.py:477
  12.6 0.0 copy-done.2
  12.6 0.0 copy-done.1
  12.6 58.5 %shard_map.104 = bf16[32,2,8,1280]{3,2,1,0:T(8,128)(2,1)S(1)} custom-call(bf16[32,8,2560]{2,1,0:T(8,128)(2,1)S(1)} %convolution_convert_fusion.refs_0_, bf16[2560,384]{1,0:T(8,128)(2,1)S(1)} %bitcast.60, bf16[192,2560]{1,0:T(8,128)(2,1)S(1)} %bitcast.61), custom_call_target="tpu_custom_call" | custom-call | bytes 200000000 | tf_op jit(solution)/shard_map/pallas_call | solution.py:295
  71.2 0.2 fusion.27
  71.4 0.0 copy-start.6
  71.4 1.4 fusion
  72.8 22.1 %shard_map.105 = bf16[8,16,1280]{2,1,0:T(8,128)(2,1)} custom-call(bf16[8,16,1280]{2,1,0:T(8,128)(2,1)} %bitcast.62), custom_call_target="tpu_custom_call" | custom-call | bytes 40000000 | tf_op jit(solution)/shard_map/pallas_call | solution.py:118
  94.9 0.0 copy-start.5
  95.0 1.7 %convert_reduce_fusion = f32[16,1280]{1,0:T(8,128)} fusion(bf16[8,16,1280]{2,1,0:T(8,128)(2,1)} %shard_map.105), kind=kLoop, calls=%fused_computation.17 | loop fusion | flops 307200 | bytes 409600 | tf_op jit(solution)/shard_map/reduce_sum | solution.py:497
  96.6 3.4 %shard_map.106 = f32[2,8,1280]{2,1,0:T(8,128)} custom-call(f32[2,8,1280]{2,1,0:T(8,128)} %bitcast.63), custom_call_target="tpu_custom_call" | custom-call | tf_op jit(solution)/shard_map/pallas_call | solution.py:338
  100.1 0.0 copy-done.6
  100.1 0.8 slice_bitcast_fusion.1
  100.9 0.9 fusion.19
  101.8 0.7 fusion.21.refs_0_
  102.5 30.9 %shard_map.107 = bf16[32,8,2560]{2,1,0:T(8,128)(2,1)} custom-call(bf16[8,2560]{1,0:T(8,128)(2,1)} %fusion.21.refs_0_), custom_call_target="tpu_custom_call" | custom-call | bytes 40000000 | tf_op jit(solution)/shard_map/pallas_call | solution.py:420
  133.5 0.0 copy-done.5
  133.5 0.1 constant_dynamic-slice_fusion
  133.6 0.1 eq.77
  133.7 0.0 all-gather.2.cloned.1.call-done
  133.7 6.4 %fusion.37 = (f32[256]{0:T(256)S(1)}, f32[256,1664]{1,0:T(8,128)S(1)}) fusion(bf16[2560,1664]{1,0:T(8,128)(2,1)} %all-gather.2.cloned.1.call-done, bf16[32,8,2560]{2,1,0:T(8,128)(2,1)} %shard_map.107), kind=kOutput, calls=%fused_computation.73 | convolution fusion | flops 2181463808 | bytes 11535360 | tf_op jit(solution)/shard_map/dot_general | solution.py:505
  140.2 0.8 exponential_reduce_fusion
  140.9 0.6 pad_maximum_fusion.refs_0_
  141.5 13.5 %shard_map.108 = f32[32,4,256]{2,1,0:T(4,128)} custom-call(f32[4,256]{1,0:T(4,128)} %pad_maximum_fusion.refs_0_), custom_call_target="tpu_custom_call" | custom-call | bytes 40000000 | tf_op jit(solution)/shard_map/pallas_call | solution.py:118
  155.1 1.3 fusion.36
  156.4 0.1 sub.70
  156.5 0.7 copy.36
  157.1 0.1 sub.72
  157.2 0.7 copy.37
  (15 shorter events, 0.2 us)
Async XLA Ops:
  7.2 2.8 %copy-start = (bf16[2560,64]{0,1:T(8,128)(2,1)S(1)}, bf16[2560,64]{0,1:T(8,128)(2,1)}, u32[]{:S(2)}) copy-start(bf16[2560,64]{0,1:T(8,128)(2,1)} %param.11) | copy-start | bytes 983044
  7.2 2.6 %copy-start.3 = (bf16[128,2560]{1,0:T(8,128)(2,1)S(1)}, bf16[128,2560]{1,0:T(8,128)(2,1)}, u32[]{:S(2)}) copy-start(bf16[128,2560]{1,0:T(8,128)(2,1)} %param.9) | copy-start | bytes 1966084
  7.2 126.5 %all-gather.2.cloned.1.call-start = ((), (), s32[]{:S(2)}) async-start(), calls=%async_computation | async-start | bytes 9052160 | tf_op jit(solution)/shard_map/all_gather | solution.py:451
  8.7 1.7 %copy-start.4 = (s32[128,6]{0,1:T(8,128)S(1)}, s32[128,6]{0,1:T(8,128)}, u32[]{:S(2)}) copy-start(s32[128,6]{0,1:T(8,128)} %param.12) | copy-start | bytes 9220
  10.0 2.7 %copy-start.2 = (bf16[1,192,2560]{2,1,0:T(8,128)(2,1)S(1)}, bf16[1,192,2560]{2,1,0:T(8,128)(2,1)}, u32[]{:S(2)}) copy-start(bf16[1,192,2560]{2,1,0:T(8,128)(2,1)} %param.14) | copy-start | bytes 2949124
  10.4 2.2 %copy-start.1 = (bf16[1,2560,384]{2,1,0:T(8,128)(2,1)S(1)}, bf16[1,2560,384]{2,1,0:T(8,128)(2,1)}, u32[]{:S(2)}) copy-start(bf16[1,2560,384]{2,1,0:T(8,128)(2,1)} %param.13) | copy-start | bytes 5898244
  71.4 28.6 %copy-start.6 = (bf16[2560]{0:T(1024)(128)(2,1)S(1)}, bf16[2560]{0:T(1024)(128)(2,1)}, u32[]{:S(2)}) copy-start(bf16[2560]{0:T(1024)(128)(2,1)} %param.15) | copy-start | bytes 15364
  94.9 38.5 %copy-start.5 = (s32[4096]{0:T(1024)S(1)}, s32[4096]{0:T(1024)}, u32[]{:S(2)}) copy-start(s32[4096]{0:T(1024)} %param.17) | copy-start | bytes 49156
Sparse Core Ops, SparseCore 0:
  10.1 73.6 all-gather.1

commit v6 on v5

--- a/solution.py
+++ b/solution.py
@@ -355,9 +355,8 @@
         return lax.rem(row + y_chips, y_chips) * X_CHIPS + lax.rem(column, X_CHIPS)
 
     above, below = at(y + 1, x), at(y - 1, x)
-    above2, below2 = at(y + 2, x), at(y - 2, x)
     right, left = at(y, x + 1), at(y, x + 3)
-    greet([{"gx": other} for other in (above, below, above2, below2, right, left)])
+    greet([{"gx": other} for other in (above, below, right, left)])
     sent = []
 
     def send(block, source, target):
@@ -380,13 +379,10 @@
 
     send(me, src, above)
     send(me, src, below)
-    send(me, src, above2)
-    send(me, src, below2)
     send(me, src, right)
     send(me, src, left)
     own = pltpu.make_async_copy(src, out.at[me], own_sem)
     own.start()
-    assert y_chips == 8
     half = y_chips // 2
     order = [0]
     for step in range(1, half + 1):
@@ -397,10 +393,9 @@
         if k:
             block = at(y + k, x)
             arrived(block)
-            if k == y_chips - 2:
-                send(block, out.at[block], above2)
+            if half < k:
                 send(block, out.at[block], above)
-            elif k == 2:
+            elif k < half - 1:
                 send(block, out.at[block], below)
             send(block, out.at[block], right)
             send(block, out.at[block], left)

time: 165 us -> 164 us (level)
  the two profiles are of different devices: /device:TPU:64 before, /device:TPU:16 now
where the time goes in v6:
time: 164 us
  Pallas kernels  128 us (78%)
  between operations  14.3 us (9%)
  matrix products  10.5 us (6%)
  other arithmetic  7.95 us (5%)
  local copies, waits for them, and re-layouts  2.69 us (2%)
    pallas_call x1, Pallas kernels, through_experts(): pl.pallas_call(functools.partial(expert_kernel, count), out_shape=jax.Sha...  56.6 us
    pallas_call x2, Pallas kernels, exchange(): pl.pallas_call(functools.partial(exchange_kernel, axis, same, count), out...  41.1 us
    pallas_call x1, Pallas kernels, relay_gather(): pl.pallas_call(functools.partial(relay_kernel, count), out_shape=jax.Shap...  26.4 us
    dot_general x1, matrix products, shards(): logits = jnp.dot(gathered, head_full, preferred_element_type=jnp.float32)  6.45 us
    pallas_call x1, Pallas kernels, pair_swap(): pl.pallas_call(pair_kernel, out_shape=jax.ShapeDtypeStruct(values.shape,...  3.44 us
  transfers between devices with their start and end apart: 1, of which 0 were waited for; matrix products, arithmetic and copies ran while one was open for 6% of the time, Pallas kernels for 68%

profile of v6, /device:TPU:16, one launch (start us, length us, event | category | flops | bytes accessed | tf_op | source)
XLA Modules:
  0.0 163.8 jit_solution(3079386111930605073)
XLA Ops:
  7.2 0.0 copy-start
  7.2 0.0 copy-start.3
  7.2 0.0 all-gather.2.cloned.1.call-start
  7.2 0.7 all-gather.2.cloned.1.call-update
  7.9 0.7 convert_reduce_fusion.1
  8.7 0.0 copy-start.4
  8.7 0.1 copy.29
  8.8 0.2 reduce_window_sum.11
  8.9 0.1 copy.31
  9.0 0.7 convert_element_type.74
  9.7 0.0 copy-done.3
  9.7 0.2 fusion.2
  10.0 0.0 copy-done
  10.0 0.0 copy-start.2
  10.0 0.4 fusion.15
  10.4 0.0 copy-done.4
  10.4 0.0 copy-start.1
  10.5 0.2 convolution_convert_fusion.1
  10.8 1.9 %convolution_convert_fusion.refs_0_ = bf16[32,8,2560]{2,1,0:T(8,128)(2,1)S(1)} fusion(bf16[128,2560]{1,0:T(8,128)(2,1)} %param.9, f32[2560]{0:T(1024)S(1)} %convert_element_type.74, f32[128]{0:T(128)S(1)} %add_rsqrt_fusion.1, bf16[32,8,128]{2,0,1:T(8,128)(2,1)S(1)} %dynamic-slice_bitcast_fusion), kind=kOutput, calls=%fused_computation | convolution fusion | flops 169738240 | bytes 2042368 | tf_op jit(solution)/shard_map/tcn,nd->tcd/dot_general | solution.py:472
  12.6 0.0 copy-done.2
  12.6 0.0 copy-done.1
  12.6 56.6 %shard_map.104 = bf16[32,2,8,1280]{3,2,1,0:T(8,128)(2,1)S(1)} custom-call(bf16[32,8,2560]{2,1,0:T(8,128)(2,1)S(1)} %convolution_convert_fusion.refs_0_, bf16[2560,384]{1,0:T(8,128)(2,1)S(1)} %bitcast.60, bf16[192,2560]{1,0:T(8,128)(2,1)S(1)} %bitcast.61), custom_call_target="tpu_custom_call" | custom-call | bytes 200000000 | tf_op jit(solution)/shard_map/pallas_call | solution.py:295
  69.3 0.2 fusion.27
  69.5 0.0 copy-start.6
  69.5 1.4 fusion
  70.9 24.8 %shard_map.105 = bf16[8,16,1280]{2,1,0:T(8,128)(2,1)} custom-call(bf16[8,16,1280]{2,1,0:T(8,128)(2,1)} %bitcast.62), custom_call_target="tpu_custom_call" | custom-call | bytes 40000000 | tf_op jit(solution)/shard_map/pallas_call | solution.py:118
  95.6 0.0 copy-start.5
  95.6 1.7 %convert_reduce_fusion = f32[16,1280]{1,0:T(8,128)} fusion(bf16[8,16,1280]{2,1,0:T(8,128)(2,1)} %shard_map.105), kind=kLoop, calls=%fused_computation.17 | loop fusion | flops 307200 | bytes 409600 | tf_op jit(solution)/shard_map/reduce_sum | solution.py:492
  97.3 3.4 %shard_map.106 = f32[2,8,1280]{2,1,0:T(8,128)} custom-call(f32[2,8,1280]{2,1,0:T(8,128)} %bitcast.63), custom_call_target="tpu_custom_call" | custom-call | tf_op jit(solution)/shard_map/pallas_call | solution.py:338
  100.8 0.0 copy-done.6
  100.8 0.8 slice_bitcast_fusion.1
  101.6 0.9 fusion.19
  102.5 0.7 fusion.21.refs_0_
  103.2 26.4 %shard_map.107 = bf16[32,8,2560]{2,1,0:T(8,128)(2,1)} custom-call(bf16[8,2560]{1,0:T(8,128)(2,1)} %fusion.21.refs_0_), custom_call_target="tpu_custom_call" | custom-call | bytes 40000000 | tf_op jit(solution)/shard_map/pallas_call | solution.py:415
  129.7 0.0 copy-done.5
  129.7 0.1 constant_dynamic-slice_fusion
  129.8 0.1 eq.77
  129.9 0.0 all-gather.2.cloned.1.call-done
  129.9 6.4 %fusion.37 = (f32[256]{0:T(256)S(1)}, f32[256,1664]{1,0:T(8,128)S(1)}) fusion(bf16[2560,1664]{1,0:T(8,128)(2,1)} %all-gather.2.cloned.1.call-done, bf16[32,8,2560]{2,1,0:T(8,128)(2,1)} %shard_map.107), kind=kOutput, calls=%fused_computation.73 | convolution fusion | flops 2181463808 | bytes 11535360 | tf_op jit(solution)/shard_map/dot_general | solution.py:500
  136.3 0.8 exponential_reduce_fusion
  137.1 0.6 pad_maximum_fusion.refs_0_
  137.7 16.4 %shard_map.108 = f32[32,4,256]{2,1,0:T(4,128)} custom-call(f32[4,256]{1,0:T(4,128)} %pad_maximum_fusion.refs_0_), custom_call_target="tpu_custom_call" | custom-call | bytes 40000000 | tf_op jit(solution)/shard_map/pallas_call | solution.py:118
  154.1 1.3 fusion.36
  155.4 0.1 sub.70
  155.5 0.7 copy.36
  156.2 0.1 sub.72
  156.2 0.7 copy.37
  (15 shorter events, 0.2 us)
Async XLA Ops:
  7.2 2.8 %copy-start = (bf16[2560,64]{0,1:T(8,128)(2,1)S(1)}, bf16[2560,64]{0,1:T(8,128)(2,1)}, u32[]{:S(2)}) copy-start(bf16[2560,64]{0,1:T(8,128)(2,1)} %param.11) | copy-start | bytes 983044
  7.2 2.6 %copy-start.3 = (bf16[128,2560]{1,0:T(8,128)(2,1)S(1)}, bf16[128,2560]{1,0:T(8,128)(2,1)}, u32[]{:S(2)}) copy-start(bf16[128,2560]{1,0:T(8,128)(2,1)} %param.9) | copy-start | bytes 1966084
  7.2 122.7 %all-gather.2.cloned.1.call-start = ((), (), s32[]{:S(2)}) async-start(), calls=%async_computation | async-start | bytes 9052160 | tf_op jit(solution)/shard_map/all_gather | solution.py:446
  8.7 1.7 %copy-start.4 = (s32[128,6]{0,1:T(8,128)S(1)}, s32[128,6]{0,1:T(8,128)}, u32[]{:S(2)}) copy-start(s32[128,6]{0,1:T(8,128)} %param.12) | copy-start | bytes 9220
  10.0 2.7 %copy-start.2 = (bf16[1,192,2560]{2,1,0:T(8,128)(2,1)S(1)}, bf16[1,192,2560]{2,1,0:T(8,128)(2,1)}, u32[]{:S(2)}) copy-start(bf16[1,192,2560]{2,1,0:T(8,128)(2,1)} %param.14) | copy-start | bytes 2949124
  10.4 2.2 %copy-start.1 = (bf16[1,2560,384]{2,1,0:T(8,128)(2,1)S(1)}, bf16[1,2560,384]{2,1,0:T(8,128)(2,1)}, u32[]{:S(2)}) copy-start(bf16[1,2560,384]{2,1,0:T(8,128)(2,1)} %param.13) | copy-start | bytes 5898244
  69.5 31.3 %copy-start.6 = (bf16[2560]{0:T(1024)(128)(2,1)S(1)}, bf16[2560]{0:T(1024)(128)(2,1)}, u32[]{:S(2)}) copy-start(bf16[2560]{0:T(1024)(128)(2,1)} %param.15) | copy-start | bytes 15364
  95.6 34.0 %copy-start.5 = (s32[4096]{0:T(1024)S(1)}, s32[4096]{0:T(1024)}, u32[]{:S(2)}) copy-start(s32[4096]{0:T(1024)} %param.17) | copy-start | bytes 49156
Sparse Core Ops, SparseCore 0:
  10.1 75.4 all-gather.1
